TPU v7x, 256 devices: a whole 4x4x8 slice. The times are simulated.
256 devices in a mesh: section: 4 (over y), ctx: 16 (over z_lo, x), tp: 4 (over z_hi, core).
Axes of the slice: x: 4, y: 4, z: 8 (z_hi: 2, z_lo: 4; z = z_hi * 4 + z_lo), core: 2. Of those that a mesh axis runs over, the one named last changes fastest.
Arguments:
- query_heads: bfloat16 [4, 2, 2048, 6144], P('section', None, 'ctx', 'tp'), may hold values from -8 to 8
- keys_values: bfloat16 [4, 2048, 2, 1024], P('section', 'ctx', None, 'tp'), may hold values from -12 to 12
- grad_output: bfloat16 [4, 2, 2048, 6144], P('section', None, 'ctx', 'tp'), may hold values from -6 to 6
- norm_gain: float32 [4, 2, 6144], P('section', None, 'tp'), may hold values from 0.1 to 1.9
- turn_ids: int32 [2048], P('ctx'), may hold values from 0 to 63, never falling along the last dimension, each value on 1 to 64 neighbouring positions
Outputs:
- normed_out: bfloat16 [4, 2, 2048, 6144], P('section', None, 'ctx', 'tp')
- query_grad: bfloat16 [4, 2, 2048, 6144], P('section', None, 'ctx', 'tp')
- kv_grad: float32 [4, 2048, 2, 1024], P('section', 'ctx', None, 'tp')
Inputs may be any that keep to these rules, and one draw needn't show every extreme that they name: `turn_ids`: turn numbers never fall along the dialogue; a turn holds 1 to 64 positions and one holds exactly 64; every turn number occurs.
All inputs are finite; a program needn't handle non-finite values.
Results may differ from a plain program's by a relative error of at most 0.015.
Values may be sent and summed in bfloat16 or wider, within the bound.
No kernel may reach another device: no remote copies, remote signals or barrier semaphores. Data moves between devices by JAX's collectives and lax.ppermute only.
A program may use at most 64 MiB of HBM per device.

v0:
```python
import jax
import jax.numpy as jnp
from jax import lax
from jax.sharding import Mesh
from jax.sharding import PartitionSpec as P

HD = 128
KVH = 8
GROUP = 6
CTX = ("ctx_0", "ctx_1")


neg_big = -1e30
eps_norm = 1e-06


def sent_to_all(x, axis):
    size = lax.axis_size(axis)
    return lax.all_to_all(jnp.broadcast_to(x[None], (size, *x.shape)), axis, 0, 0, tiled=True)


def of_everyone(x, axis):
    return sent_to_all(x, axis).sum(axis=0)


def in_one(arrays, axis):
    ends = [0]
    for a in arrays:
        ends.append(ends[-1] + a.size)
    running = of_everyone(jnp.concatenate([a.ravel() for a in arrays]), axis)
    return tuple((running[b:e].reshape(a.shape) for a, b, e in zip(arrays, ends, ends[1:])))


def passed_along(block, axis, distance):
    devices = range(lax.axis_size(axis))
    route = [((i - distance) % len(devices), i) for i in devices]
    return lax.ppermute(block, axis, route)


def in_order(parts, dim):
    shape = list(parts.shape[1:])
    shape[dim] *= parts.shape[0]
    return jnp.moveaxis(parts, 0, dim).reshape(shape)


def collect(x, axis, dim):
    return in_order(sent_to_all(x, axis), dim)


def reduced_to_own(parts, axes, order):
    shape = [lax.axis_size(a) for a in axes]
    parts = parts.reshape(*shape, *parts.shape[1:])
    parts = parts.transpose(*order, *range(len(axes), parts.ndim))
    parts = parts.reshape(-1, *parts.shape[len(axes) :])
    for k in order:
        parts = lax.psum_scatter(parts, axes[k], scatter_dimension=0, tiled=True)
    return parts[0]


def split_up(x, dim, size):
    shape = x.shape
    parts = x.reshape(*shape[:dim], size, shape[dim] // size, *shape[dim + 1 :])
    return jnp.moveaxis(parts, dim, 0)


def scatter_axes(x, axes, order, dim):
    size = lax.axis_size(axes)
    return reduced_to_own(split_up(x, dim, size), axes, order)


def visible_mask(query_pos, query_seg, key_pos, key_seg):
    return (key_pos[None, :] <= query_pos[:, None]) | (key_seg[None, :] == query_seg[:, None])


def block_terms(queries, kv_rows, scaling):
    row_count = kv_rows.shape[0]
    head_count = queries.shape[1]
    key_rows = kv_rows[:, 0].reshape(row_count, head_count, HD)
    value_rows = kv_rows[:, 1].reshape(row_count, head_count, HD)
    scores = (
        jnp.einsum("qhgd,khd->hgqk", queries, key_rows, preferred_element_type=jnp.float32)
        * scaling
    )
    return (scores, key_rows, value_rows)


def run_layer(queries_flat, gathered, key_seg, query_pos, query_seg, gain_vector, cotangent_flat):
    tokens_here = queries_flat.shape[0]
    head_count = gathered.shape[2] // HD
    queries = queries_flat.reshape(tokens_here, head_count, GROUP, HD)
    scaling = HD ** (-0.5)
    seq_len = gathered.shape[0]
    span_rows = min(512, seq_len)
    blocks = seq_len // span_rows

    def block_view(number):
        offset = number * span_rows
        kv_rows = lax.dynamic_slice_in_dim(gathered, offset, span_rows, 0)
        key_pos = offset + jnp.arange(span_rows, dtype=jnp.int32)
        visible = visible_mask(
            query_pos, query_seg, key_pos, lax.dynamic_slice_in_dim(key_seg, offset, span_rows, 0)
        )
        scores, key_rows, value_rows = block_terms(queries, kv_rows, scaling)
        return (scores, key_rows, value_rows, visible)

    def forward_step(running, number):
        run_max, run_sum, accumulated = running
        scores, key_rows, value_rows, visible = block_view(number)
        new_max = jnp.maximum(run_max, jnp.max(jnp.where(visible, scores, neg_big), axis=-1))
        weights = jnp.where(visible, jnp.exp(scores - new_max[..., None]), 0.0)
        factor = jnp.exp(run_max - new_max)
        run_sum = run_sum * factor + jnp.sum(weights, axis=-1)
        update = jnp.einsum(
            "hgqk,khd->qhgd",
            weights.astype(jnp.bfloat16),
            value_rows,
            preferred_element_type=jnp.float32,
        )
        accumulated = accumulated * jnp.transpose(factor, (2, 0, 1))[..., None] + update
        return ((new_max, run_sum, accumulated), None)

    start_state = (
        jnp.full((head_count, GROUP, tokens_here), neg_big, jnp.float32),
        jnp.zeros((head_count, GROUP, tokens_here), jnp.float32),
        jnp.zeros((tokens_here, head_count, GROUP, HD), jnp.float32),
    )
    (row_max, row_sum, accumulated), unused = lax.scan(
        forward_step, start_state, jnp.arange(blocks, dtype=jnp.int32)
    )
    output = accumulated / jnp.transpose(row_sum, (2, 0, 1))[..., None]
    gain_grid = gain_vector.reshape(head_count, GROUP, HD)
    scaled = (
        cotangent_flat.reshape(tokens_here, head_count, GROUP, HD).astype(jnp.float32) * gain_grid
    )
    local_sq = jnp.sum(output * output, axis=(1, 2, 3))
    local_dot = jnp.sum(scaled * output, axis=(1, 2, 3))
    total_sq, total_dot = in_one((local_sq, local_dot), "tp")
    features = KVH * GROUP * HD
    inverse = lax.rsqrt(total_sq / features + eps_norm)
    normed = (output * inverse[:, None, None, None] * gain_grid).astype(jnp.bfloat16)
    center = total_dot / features
    out_grad = (
        inverse[:, None, None, None]
        * (scaled - output * (inverse * inverse * center)[:, None, None, None])
    ).astype(jnp.bfloat16)
    row_dot = jnp.transpose(jnp.sum(out_grad.astype(jnp.float32) * output, axis=-1), (1, 2, 0))

    def backward_step(grad_q, number):
        scores, key_rows, value_rows, visible = block_view(number)
        chances = jnp.where(visible, jnp.exp(scores - row_max[..., None]), 0.0) / row_sum[..., None]
        value_grad = jnp.einsum(
            "hgqk,qhgd->khd",
            chances.astype(jnp.bfloat16),
            out_grad,
            preferred_element_type=jnp.float32,
        )
        prob_grad = jnp.einsum(
            "qhgd,khd->hgqk", out_grad, value_rows, preferred_element_type=jnp.float32
        )
        score_grad = (chances * (prob_grad - row_dot[..., None])).astype(jnp.bfloat16)
        grad_q = (
            grad_q
            + jnp.einsum("hgqk,khd->qhgd", score_grad, key_rows, preferred_element_type=jnp.float32)
            * scaling
        )
        key_grad = (
            jnp.einsum("hgqk,qhgd->khd", score_grad, queries, preferred_element_type=jnp.float32)
            * scaling
        )
        return (grad_q, jnp.stack([key_grad, value_grad], axis=1))

    grad_q, pieces = lax.scan(
        backward_step,
        jnp.zeros((tokens_here, head_count, GROUP, HD), jnp.float32),
        jnp.arange(blocks, dtype=jnp.int32),
    )
    kv_partial = pieces.reshape(seq_len, 2, head_count * HD)
    return (
        normed.reshape(tokens_here, -1),
        grad_q.reshape(tokens_here, -1).astype(jnp.bfloat16),
        kv_partial,
    )


def on_device(query_heads, keys_values, grad_output, norm_gain, turn_ids):
    tokens_here = turn_ids.shape[0]
    query_pos = lax.axis_index(CTX) * tokens_here + jnp.arange(tokens_here, dtype=jnp.int32)
    own_rows = keys_values[0]
    earlier = passed_along(own_rows, "section", 1)
    own_full, key_seg = (collect(own_rows, CTX, 0), collect(turn_ids, CTX, 0))
    earlier_full = collect(earlier, CTX, 0)
    producer = run_layer(
        query_heads[0, 0],
        own_full,
        key_seg,
        query_pos,
        turn_ids,
        norm_gain[0, 0],
        grad_output[0, 0],
    )
    consumer = run_layer(
        query_heads[0, 1],
        earlier_full,
        key_seg,
        query_pos,
        turn_ids,
        norm_gain[0, 1],
        grad_output[0, 1],
    )
    normed = jnp.stack([producer[0], consumer[0]])[None]
    grad_q = jnp.stack([producer[1], consumer[1]])[None]
    returned = passed_along(consumer[2].astype(jnp.bfloat16), "section", -1).astype(jnp.float32)
    kv_grad = scatter_axes(producer[2] + returned, CTX, (1, 0), 0)
    return (normed, grad_q, kv_grad[None])


def solution(mesh):
    split = Mesh(
        mesh.devices.reshape(mesh.shape["section"], 4, 4, mesh.shape["tp"]),
        ("section", "ctx_0", "ctx_1", "tp"),
    )
    return jax.shard_map(
        on_device,
        mesh=split,
        in_specs=(
            P("section", None, CTX, "tp"),
            P("section", CTX, None, "tp"),
            P("section", None, CTX, "tp"),
            P("section", None, "tp"),
            P(CTX),
        ),
        out_specs=(
            P("section", None, CTX, "tp"),
            P("section", None, CTX, "tp"),
            P("section", CTX, None, "tp"),
        ),
        check_vma=False,
    )
```

profile of v0, /device:TPU:4, one launch (start us, length us, event | category | flops | bytes accessed | tf_op | source)
XLA Modules:
  0.0 401.3 jit_solution(3898352928093799559)
XLA Ops:
  10.0 9.0 %all-to-all-start.1 = ((bf16[16,128,2,256]{1,3,2,0:T(8,128)(2,1)}), bf16[16,128,2,256]{1,3,2,0:T(8,128)(2,1)S(1)}, u32[]{:S(2)}, u32[]{:S(2)}) async-start(bf16[16,128,2,256]{1,3,2,0:T(8,128)(2,1)} %broadcast_in_dim.85), calls=%async_computation.1 | async-start | bytes 4194304 | tf_op jit(solution)/shard_map/all_to_all | solution.py:19
  21.5 1.9 fusion.91
  23.5 39.4 %all-to-all-done.1 = bf16[16,128,2,256]{1,3,2,0:T(8,128)(2,1)S(1)} async-done(((bf16[16,128,2,256]{1,3,2,0:T(8,128)(2,1)}), bf16[16,128,2,256]{1,3,2,0:T(8,128)(2,1)S(1)}, u32[]{:S(2)}, u32[]{:S(2)}) %all-to-all-start.1) | async-done | bytes 2097184 | tf_op jit(solution)/shard_map/all_to_all | solution.py:19
  63.5 9.6 %all-to-all-start = ((s32[16,1,128]{2,1,0:T(1,128)}), s32[16,1,128]{2,1,0:T(1,128)S(1)}, u32[]{:S(2)}, u32[]{:S(2)}) async-start(s32[16,1,128]{2,1,0:T(1,128)} %broadcast_in_dim.76), calls=%async_computation | async-start | bytes 16384 | tf_op jit(solution)/shard_map/all_to_all | solution.py:19
  73.8 2.6 copy.183
  76.4 2.9 copy.185
  79.4 19.2 %while.56 = (s32[]{:T(128)}, f32[2,6,128]{2,1,0:T(8,128)S(1)}, f32[2,6,128]{2,1,0:T(8,128)S(1)}, f32[128,2,6,128]{0,3,2,1:T(8,128)}, s32[4]{0:T(128)S(1)}, /*ind...) while((s32[]{:T(128)}, f32[2,6,128]{2,1,0:T(8,128)S(1)}, ...), condition=%wide.region_3.4_spmd.clone, body=%wide.region_0.3_spmd.clone.sunk | while | flops 412100224 | bytes 19640116 | solution.py:127
  98.6 2.0 multiply_reduce_fusion.3
  101.2 5.7 %all-to-all-start.2 = ((f32[4,1,256]{2,1,0:T(1,128)}), f32[4,1,256]{2,1,0:T(1,128)S(1)}, u32[]{:S(2)}, u32[]{:S(2)}) async-start(f32[4,1,256]{2,1,0:T(1,128)} %broadcast_in_dim.86), calls=%async_computation.2 | async-start | bytes 8192 | tf_op jit(solution)/shard_map/all_to_all | solution.py:19
  108.0 6.7 %all-to-all-done.2 = f32[4,1,256]{2,1,0:T(1,128)S(1)} async-done(((f32[4,1,256]{2,1,0:T(1,128)}), f32[4,1,256]{2,1,0:T(1,128)S(1)}, u32[]{:S(2)}, u32[]{:S(2)}) %all-to-all-start.2) | async-done | bytes 4128 | tf_op jit(solution)/shard_map/all_to_all | solution.py:19
  116.4 7.5 %all-to-all-start.3 = ((bf16[16,128,2,256]{1,3,2,0:T(8,128)(2,1)}), bf16[16,128,2,256]{1,3,2,0:T(8,128)(2,1)}, u32[]{:S(2)}, u32[]{:S(2)}) async-start(bf16[16,128,2,256]{1,3,2,0:T(8,128)(2,1)} %broadcast_in_dim.116), calls=%async_computation.3 | async-start | bytes 4194304 | tf_op jit(solution)/shard_map/all_to_all | solution.py:19
  126.8 41.1 %all-to-all-done.3 = bf16[16,128,2,256]{1,3,2,0:T(8,128)(2,1)} async-done(((bf16[16,128,2,256]{1,3,2,0:T(8,128)(2,1)}), bf16[16,128,2,256]{1,3,2,0:T(8,128)(2,1)}, u32[]{:S(2)}, u32[]{:S(2)}) %all-to-all-start.3) | async-done | bytes 2097184 | tf_op jit(solution)/shard_map/all_to_all | solution.py:19
  167.8 3.9 copy.190
  171.8 4.0 copy.192
  175.8 23.3 %while.57 = (s32[]{:T(128)}, f32[2,6,128]{2,1,0:T(8,128)S(1)}, f32[2,6,128]{2,1,0:T(8,128)S(1)}, f32[128,2,6,128]{0,3,2,1:T(8,128)}, s32[4]{0:T(128)S(1)}, /*ind...) while((s32[]{:T(128)}, f32[2,6,128]{2,1,0:T(8,128)S(1)}, ...), condition=%wide.region_10.11_spmd.clone, body=%wide.region_7.0_spmd.clone.sunk | while | flops 412100224 | bytes 19640116 | solution.py:127
  201.1 3.2 all-to-all-start.4
  204.6 2.4 multiply_reduce_fusion.1
  208.2 3.8 all-to-all-done.4
  212.0 2.4 multiply_reduce_fusion
  215.7 27.1 %while.59 = (s32[]{:T(128)}, f32[128,2,6,128]{0,3,2,1:T(8,128)S(1)}, bf16[4,512,2,2,128]{4,1,3,2,0:T(8,128)(2,1)}, s32[4]{0:T(128)S(1)}, bf16[2048,2,256]{0,2,1:...) while((s32[]{:T(128)}, ...), condition=%wide.region_19.20_spmd.clone, body=%wide.region_18.19_spmd.clone.sunk | while | flops 1015022208 | bytes 20870932 | solution.py:172
  242.8 5.1 %copy.203 = bf16[4,512,2,2,128]{4,3,1,0,2:T(2,128)(2,1)} copy(bf16[4,512,2,2,128]{4,1,3,2,0:T(8,128)(2,1)} %get-tuple-element.256) | data formatting | bytes 4194304 | tf_op jit(solution)/shard_map/convert_element_type | solution.py:212
  247.9 4.4 %convert_element_type.98 = bf16[2048,2,256]{2,0,1:T(8,128)(2,1)} reshape(bf16[4,512,2,2,128]{4,3,1,0,2:T(2,128)(2,1)} %copy.203) | data formatting | bytes 4194304 | tf_op jit(solution)/shard_map/convert_element_type | solution.py:212
  252.3 3.0 collective-permute-start.1
  255.3 31.2 %while.58 = (s32[]{:T(128)}, f32[128,2,6,128]{0,3,2,1:T(8,128)S(1)}, f32[4,512,2,2,128]{4,3,1,0,2:T(2,128)}, s32[4]{0:T(128)S(1)}, bf16[2048,2,256]{0,2,1:T(8,12...) while((s32[]{:T(128)}, ...), condition=%wide.region_16.17_spmd.clone, body=%wide.region_15.16_spmd.clone.sunk | while | flops 1014104704 | bytes 24540948 | solution.py:172
  269.1 1.8 copy_dynamic-update-slice_fusion.2
  286.5 6.4 %reshape.128 = f32[2048,2,256]{2,0,1:T(8,128)} reshape(f32[4,512,2,2,128]{4,3,1,0,2:T(2,128)} %get-tuple-element.255) | data formatting | bytes 8388608 | tf_op jit(solution)/shard_map/reshape | solution.py:177
  292.9 7.5 %collective-permute-done.1 = bf16[2048,2,256]{2,0,1:T(8,128)(2,1)} collective-permute-done((bf16[2048,2,256]{2,0,1:T(8,128)(2,1)}, bf16[2048,2,256]{2,0,1:T(8,128)(2,1)}, u32[]{:S(2)}, u32[]{:S(2)}) %collective-permute-start.1) | collective-permute-done | bytes 2097184 | tf_op jit(solution)/shard_map/ppermute | solution.py:37
  300.5 3.3 convert_add_fusion
  303.8 2.2 copy.204
  306.0 50.1 %reduce-scatter.3.cloned.1.call-done = f32[4,128,2,256]{3,1,2,0:T(8,128)} async-done(((f32[16,128,2,256]{3,1,2,0:T(8,128)}), f32[4,128,2,256]{3,1,2,0:T(8,128)}) %reduce-scatter.3.cloned.1.call-update) | async-done | bytes 1048592 | tf_op jit(solution)/shard_map/reduce_scatter | solution.py:56
  358.8 33.8 %reduce-scatter.5.cloned.1.call-done = f32[1,128,2,256]{3,1,2,0:T(8,128)} async-done(((f32[4,128,2,256]{3,1,2,0:T(8,128)}), f32[1,128,2,256]{3,1,2,0:T(8,128)}) %reduce-scatter.5.cloned.1.call-update) | async-done | bytes 262160 | tf_op jit(solution)/shard_map/reduce_scatter | solution.py:56
  392.6 1.9 copy.207
  (294 shorter events, 107.5 us)
Async XLA Ops:
  8.2 10.9 %copy-start.9 = (bf16[1,128,2,256]{3,2,1,0:T(2,128)(2,1)S(1)}, bf16[1,128,2,256]{3,2,1,0:T(2,128)(2,1)}, u32[]{:S(2)}) copy-start(bf16[1,128,2,256]{3,2,1,0:T(2,128)(2,1)} %param.14) | copy-start | bytes 393220
  8.2 12.5 %copy-start.7 = (bf16[1,2,128,1536]{3,2,1,0:T(8,128)(2,1)S(1)}, bf16[1,2,128,1536]{3,2,1,0:T(8,128)(2,1)}, u32[]{:S(2)}) copy-start(bf16[1,2,128,1536]{3,2,1,0:T(8,128)(2,1)} %param.13) | copy-start | bytes 2359300
  10.0 52.8 %copy-start.8 = (s32[128]{0:T(128)S(1)}, s32[128]{0:T(128)}, u32[]{:S(2)}) copy-start(s32[128]{0:T(128)} %param.17) | copy-start | bytes 1540
  10.0 63.0 %copy-start.10 = (f32[1,2,1536]{2,1,0:T(2,128)S(1)}, f32[1,2,1536]{2,1,0:T(2,128)}, u32[]{:S(2)}) copy-start(f32[1,2,1536]{2,1,0:T(2,128)} %param.16) | copy-start | bytes 36868
  10.0 52.8 %all-to-all-start.1 = ((bf16[16,128,2,256]{1,3,2,0:T(8,128)(2,1)}), bf16[16,128,2,256]{1,3,2,0:T(8,128)(2,1)S(1)}, u32[]{:S(2)}, u32[]{:S(2)}) async-start(bf16[16,128,2,256]{1,3,2,0:T(8,128)(2,1)} %broadcast_in_dim.85), calls=%async_computation.1 | async-start | bytes 4194304 | tf_op jit(solution)/shard_map/all_to_all | solution.py:19
  19.1 87.9 %collective-permute-start = (bf16[128,2,256]{2,1,0:T(2,128)(2,1)S(1)}, bf16[128,2,256]{2,1,0:T(2,128)(2,1)}, u32[]{:S(2)}, u32[]{:S(2)}) collective-permute-start(bf16[128,2,256]{2,1,0:T(2,128)(2,1)S(1)} %bitcast.382), channel_id=1, source_target_pairs={{192,0},{0,64},{64,128},{128,192},{193,1},{1,65},{65,129},{129,193... | collective-permute-start | bytes 393224 | tf_op jit(solution)/shard_map/ppermute | solution.py:37
  63.5 15.9 %all-to-all-start = ((s32[16,1,128]{2,1,0:T(1,128)}), s32[16,1,128]{2,1,0:T(1,128)S(1)}, u32[]{:S(2)}, u32[]{:S(2)}) async-start(s32[16,1,128]{2,1,0:T(1,128)} %broadcast_in_dim.76), calls=%async_computation | async-start | bytes 16384 | tf_op jit(solution)/shard_map/all_to_all | solution.py:19
  81.0 1.4 copy-start.1
  83.3 0.9 copy-start.2
  85.8 1.4 copy-start.1
  88.1 0.9 copy-start.2
  90.6 1.4 copy-start.1
  92.9 0.9 copy-start.2
  95.4 1.4 copy-start.1
  97.7 0.9 copy-start.2
  98.6 17.8 %copy-start = (bf16[2048,2,256]{0,2,1:T(8,128)(2,1)}, bf16[2048,2,256]{0,2,1:T(8,128)(2,1)S(1)}, u32[]{:S(2)}) copy-start(bf16[2048,2,256]{0,2,1:T(8,128)(2,1)S(1)} %get-tuple-element.1375) | copy-start | bytes 6291460
  101.2 13.4 %all-to-all-start.2 = ((f32[4,1,256]{2,1,0:T(1,128)}), f32[4,1,256]{2,1,0:T(1,128)S(1)}, u32[]{:S(2)}, u32[]{:S(2)}) async-start(f32[4,1,256]{2,1,0:T(1,128)} %broadcast_in_dim.86), calls=%async_computation.2 | async-start | bytes 8192 | tf_op jit(solution)/shard_map/all_to_all | solution.py:19
  116.4 51.4 %all-to-all-start.3 = ((bf16[16,128,2,256]{1,3,2,0:T(8,128)(2,1)}), bf16[16,128,2,256]{1,3,2,0:T(8,128)(2,1)}, u32[]{:S(2)}, u32[]{:S(2)}) async-start(bf16[16,128,2,256]{1,3,2,0:T(8,128)(2,1)} %broadcast_in_dim.116), calls=%async_computation.3 | async-start | bytes 4194304 | tf_op jit(solution)/shard_map/all_to_all | solution.py:19
  178.4 1.4 copy-start.3
  180.7 0.9 copy-start.4
  184.2 1.4 copy-start.3
  186.5 0.9 copy-start.4
  190.0 1.4 copy-start.3
  192.3 0.9 copy-start.4
  195.9 1.4 copy-start.3
  198.2 0.9 copy-start.4
  201.1 10.9 %all-to-all-start.4 = ((f32[4,1,256]{2,1,0:T(1,128)}), f32[4,1,256]{2,1,0:T(1,128)S(1)}, u32[]{:S(2)}, u32[]{:S(2)}) async-start(f32[4,1,256]{2,1,0:T(1,128)} %broadcast_in_dim.117), calls=%async_computation.4 | async-start | bytes 8192 | tf_op jit(solution)/shard_map/all_to_all | solution.py:19
  204.3 151.8 %reduce-scatter.3.cloned.1.call-start = ((), (), s32[]{:S(2)}) async-start(), calls=%async_computation.7 | async-start | bytes 5242880 | tf_op jit(solution)/shard_map/reduce_scatter | solution.py:56
  252.3 48.2 %collective-permute-start.1 = (bf16[2048,2,256]{2,0,1:T(8,128)(2,1)}, bf16[2048,2,256]{2,0,1:T(8,128)(2,1)}, u32[]{:S(2)}, u32[]{:S(2)}) collective-permute-start(bf16[2048,2,256]{2,0,1:T(8,128)(2,1)} %convert_element_type.98), channel_id=1, source_target_pairs={{64,0},{128,64},{192,128},{0,192},{65,1},{129,65},{193,129},{1,193... | collective-permute-start | bytes 6291464 | tf_op jit(solution)/shard_map/ppermute | solution.py:37
  306.0 50.3 %copy-start.5 = (bf16[128,2,6,128]{0,3,2,1:T(8,128)(2,1)S(1)}, bf16[128,2,6,128]{0,3,2,1:T(8,128)(2,1)}, u32[]{:S(2)}) copy-start(bf16[128,2,6,128]{0,3,2,1:T(8,128)(2,1)} %get-tuple-element.851) | copy-start | bytes 1179652
  306.0 50.3 %copy-start.6 = (bf16[128,2,6,128]{0,3,2,1:T(8,128)(2,1)S(1)}, bf16[128,2,6,128]{0,3,2,1:T(8,128)(2,1)}, u32[]{:S(2)}) copy-start(bf16[128,2,6,128]{0,3,2,1:T(8,128)(2,1)} %get-tuple-element.852) | copy-start | bytes 1179652
  306.0 86.6 %reduce-scatter.5.cloned.1.call-start = ((), (), s32[]{:S(2)}) async-start(), calls=%async_computation.8 | async-start | bytes 1310720 | tf_op jit(solution)/shard_map/reduce_scatter | solution.py:56
Sparse Core Ops, SparseCore 0:
  306.1 49.9 reduce-scatter.2
  358.7 33.8 reduce-scatter.4
where the time goes:
time: 403 us; the launch traced here: 401 us
  waiting for transfers between devices  182 us (45%)
  local copies, waits for them, and re-layouts  89.6 us (22%)
  starting transfers between devices  40 us (10%)
  matrix products  38.8 us (10%)
  other arithmetic  24.4 us (6%)
  between operations  14.4 us (4%)
  loops' own time  11.6 us (3%)
    all_to_all x5, waiting for transfers between devices, sent_to_all(): lax.all_to_all(jnp.broadcast_to(x[None], (size, *x.shape)), axis, 0, 0, t...  90.9 us
    reduce_scatter x2, waiting for transfers between devices, reduced_to_own(): parts = lax.psum_scatter(parts, axes[k], scatter_dimension=0, tiled=True)  83.9 us
    all_to_all x5, starting transfers between devices, sent_to_all(): lax.all_to_all(jnp.broadcast_to(x[None], (size, *x.shape)), axis, 0, 0, t...  35.1 us
    unnamed x27, local copies, waits for them, and re-layouts  16.9 us
    dot_general x16, matrix products, block_terms(): jnp.einsum('qhgd,khd->hgqk', queries, key_rows, preferred_element_type=jn...  13.1 us
    slice x16, local copies, waits for them, and re-layouts, block_terms(): value_rows = kv_rows[:, 1].reshape(row_count, head_count, HD)  13.1 us
    convert_element_type x2, local copies, waits for them, and re-layouts, on_device(): consumer[2].astype(jnp.bfloat16)  9.5 us
    dynamic_slice x16, local copies, waits for them, and re-layouts, run_layer(): lax.scan(forward_step, start_state, jnp.arange(blocks, dtype=jnp.int32))  9.47 us
  transfers between devices with their start and end apart: 9, of which 7 were waited for; matrix products, arithmetic and copies ran while one was open for 17% of the time, Pallas kernels for 0%

commit v1 on v0

v1 whole, which is shorter than its diff:
```python
import math

import jax
import jax.numpy as jnp
from jax import lax
from jax.experimental import pallas as pl
from jax.experimental.pallas import tpu as pltpu
from jax.sharding import Mesh
from jax.sharding import PartitionSpec as P

HD = 128
KVH = 8
GROUP = 6
FEATURES = KVH * GROUP * HD
CTX = ("ctx_0", "ctx_1")
OWN, HALO, PAST = 512, 128, 512
WIDTH = OWN + HALO + 3 * PAST
SCALE = HD**-0.5
SCALE_LOG2 = SCALE * math.log2(math.e)

neg_big = -1e30
eps_norm = 1e-06
bf16 = jnp.bfloat16
f32 = jnp.float32


def dot_nt(a, b):
    return lax.dot_general(a, b, (((1,), (1,)), ((), ())), preferred_element_type=f32)


def dot_nn(a, b):
    return lax.dot_general(a, b, (((1,), (0,)), ((), ())), preferred_element_type=f32)


def slot(x, d):
    return pl.ds(pl.multiple_of(((x - d) & 3) * 128, 128), 128)


def column_of(row):
    return jnp.transpose(jnp.broadcast_to(row, (128, 128)))


def order_kernel(info, a0, a1, a2, a3, own, first, turns):
    x = info[0]
    for d, ref in enumerate((a0, a1, a2, a3)):
        rows = slot(x, d)
        own[0, rows, :] = ref[0:128, :]
        own[1, rows, :] = ref[128:256, :]
        at = (x - d) & 3
        turns[pl.ds(at, 1), :] = ref[256:272, :].astype(f32)[0:1, :]

        @pl.when(at == 0)
        def _():
            first[...] = ref[...]


def put_in_order(info, parts):
    whole = pl.BlockSpec(memory_space=pltpu.VMEM)
    return pl.pallas_call(
        order_kernel,
        name="order_keys",
        in_specs=[pl.BlockSpec(memory_space=pltpu.SMEM)] + [whole] * 4,
        out_specs=[whole] * 3,
        out_shape=[
            jax.ShapeDtypeStruct((2, 512, 128), bf16),
            jax.ShapeDtypeStruct((272, 128), bf16),
            jax.ShapeDtypeStruct((8, 128), f32),
        ],
    )(info, *parts)


def forward_kernel(
    info, q0, q1, q2, q3, turns, own, halo, p1, p2, p3, o_ref, l_ref, e_ref, q_s, s_s, t_s
):
    x, z = info[0], info[1]
    for d, ref in enumerate((q0, q1, q2, q3)):
        q_s[slot(x, d), :] = ref[...]

    @pl.when(pl.program_id(0) == 0)
    def _():
        for c in range(4):
            t_s[128 * c : 128 * c + 128, :] = column_of(turns[c : c + 1, :])

    past = (p1, p2, p3)
    halo_turns = halo[256:272, :].astype(f32)[0:1, :]

    def masked(s, b, first_key, count):
        tiles = []
        row = 256 * b + lax.broadcasted_iota(jnp.int32, (256, 128), 0)
        lane = lax.broadcasted_iota(jnp.int32, (256, 128), 1)
        mine = t_s[256 * b : 256 * b + 256, :]
        for j in range(count // 128):
            c = first_key // 128 + j
            theirs = turns[c : c + 1, :] if c < 4 else halo_turns
            seen = (lane + 128 * c <= row) | (mine == theirs)
            tiles.append(jnp.where(seen, s[:, 128 * j : 128 * j + 128], neg_big))
        return jnp.concatenate(tiles, axis=1)

    def block(b, reach):
        rows = pl.ds(256 * b, 256)
        q = q_s[rows, :]
        spans = []
        if b == 1:
            spans.append((own, 0, 256, 0, False))
        spans.append((own, 256 * b, 384 - 128 * b, 256 * b, True) if b == 0 else (own, 256, 256, 256, True))
        if b == 1:
            spans.append((halo, 0, 128, OWN, True))
        for d in range(reach):
            spans.append((past[d], 0, 512, OWN + HALO + 512 * d, False))
        top = None
        for ref, k0, n, c0, partial in spans:
            keys = ref[0:128, :] if ref is halo else ref[0, k0 : k0 + n, :]
            s = dot_nt(q, keys)
            if partial:
                s = masked(s, b, c0, n)
            s_s[rows, c0 : c0 + n] = s
            for j in range(n // 128):
                t = s[:, 128 * j : 128 * j + 128]
                top = t if top is None else jnp.maximum(top, t)
        top = jnp.max(top, axis=1, keepdims=True) * SCALE_LOG2
        total = mixed = None
        for ref, k0, n, c0, _ in spans:
            e = jnp.exp2(s_s[rows, c0 : c0 + n] * SCALE_LOG2 - top)
            for j in range(n // 128):
                t = e[:, 128 * j : 128 * j + 128]
                total = t if total is None else total + t
            e = e.astype(bf16)
            e_ref[0, rows, c0 : c0 + n] = e
            values = ref[128:256, :] if ref is halo else ref[1, k0 : k0 + n, :]
            t = dot_nn(e, values)
            mixed = t if mixed is None else mixed + t
        total = jnp.sum(total, axis=1, keepdims=True)
        o_ref[rows, :] = mixed / total
        l_ref[rows, :] = jnp.broadcast_to(total, (256, 128))

    for reach in range(4):

        @pl.when(z == reach)
        def _():
            block(0, reach)
            block(1, reach)


def per_head(rows):
    return pl.BlockSpec((rows, 128), lambda g, i: (0, g))


def all_of(*shape):
    return pl.BlockSpec(shape, lambda g, i: (0,) * len(shape))


def forward(info, queries, turns, own, halo, past):
    return pl.pallas_call(
        forward_kernel,
        name="attention_forward",
        grid_spec=pltpu.PrefetchScalarGridSpec(
            num_scalar_prefetch=1,
            grid=(GROUP,),
            in_specs=[per_head(128)] * 4
            + [all_of(8, 128), all_of(2, 512, 128), all_of(272, 128)]
            + [all_of(2, 512, 128)] * 3,
            out_specs=[
                per_head(512),
                per_head(512),
                pl.BlockSpec((1, 512, WIDTH), lambda g, i: (g, 0, 0)),
            ],
            scratch_shapes=[
                pltpu.VMEM((512, 128), bf16),
                pltpu.VMEM((512, WIDTH), f32),
                pltpu.VMEM((512, 128), f32),
            ],
        ),
        out_shape=[
            jax.ShapeDtypeStruct((512, GROUP * HD), f32),
            jax.ShapeDtypeStruct((512, GROUP * HD), f32),
            jax.ShapeDtypeStruct((GROUP, 512, WIDTH), bf16),
        ],
    )(info, *queries, turns, own, halo, *past)


def sums_kernel(info, o_ref, g0, g1, g2, g3, gain_ref, out):
    x = info[0]
    for d, ref in enumerate((g0, g1, g2, g3)):
        square = dotted = None
        rows = slot(x, d)
        for g in range(GROUP):
            at = pl.ds(128 * g, 128)
            o = o_ref[rows, at]
            u = ref[:, at].astype(f32) * gain_ref[:, at]
            square = o * o if square is None else square + o * o
            dotted = u * o if dotted is None else dotted + u * o
        c = (x - d) & 3
        out[pl.ds(c, 1), :] = jnp.sum(jnp.transpose(square), axis=0, keepdims=True)
        out[pl.ds(4 + c, 1), :] = jnp.sum(jnp.transpose(dotted), axis=0, keepdims=True)


def token_sums(info, output, cotangents, gain):
    whole = pl.BlockSpec(memory_space=pltpu.VMEM)
    return pl.pallas_call(
        sums_kernel,
        name="token_sums",
        in_specs=[pl.BlockSpec(memory_space=pltpu.SMEM)] + [whole] * 6,
        out_specs=whole,
        out_shape=jax.ShapeDtypeStruct((8, 128), f32),
    )(info, output, *cotangents, gain)


def normed_kernel(info, o_ref, sums, gain_ref, n0, n1, n2, n3):
    x = info[0]
    for d, ref in enumerate((n0, n1, n2, n3)):
        c = (x - d) & 3
        inverse = column_of(lax.rsqrt(sums[pl.ds(c, 1), :] / FEATURES + eps_norm))
        rows = slot(x, d)
        for g in range(GROUP):
            at = pl.ds(128 * g, 128)
            ref[:, at] = (o_ref[rows, at] * inverse * gain_ref[:, at]).astype(bf16)


def normed_parts(info, output, sums, gain):
    whole = pl.BlockSpec(memory_space=pltpu.VMEM)
    return pl.pallas_call(
        normed_kernel,
        name="normed_parts",
        in_specs=[pl.BlockSpec(memory_space=pltpu.SMEM)] + [whole] * 3,
        out_specs=[whole] * 4,
        out_shape=[jax.ShapeDtypeStruct((128, GROUP * HD), bf16)] * 4,
    )(info, output, sums, gain)


def backward_kernel(
    info, q0, q1, q2, q3, g0, g1, g2, g3, gain_ref, sums, o_ref, l_ref, e_ref,
    own, halo, p1, p2, p3,
    dq0, dq1, dq2, dq3, d_own, d_halo, d_p1, d_p2, d_p3,
    q_s, g_s, dq_s, dk_s, dv_s, r_s, c_s,
):
    x, z = info[0], info[1]
    head = pl.program_id(0)
    for d, (a, b) in enumerate(((q0, g0), (q1, g1), (q2, g2), (q3, g3))):
        q_s[slot(x, d), :] = a[...]
        g_s[slot(x, d), :] = b[...]

    @pl.when(head == 0)
    def _():
        dk_s[...] = jnp.zeros_like(dk_s)
        dv_s[...] = jnp.zeros_like(dv_s)
        for c in range(4):
            inverse = lax.rsqrt(sums[c : c + 1, :] / FEATURES + eps_norm)
            center = sums[4 + c : 5 + c, :] / FEATURES
            r_s[128 * c : 128 * c + 128, :] = column_of(inverse)
            c_s[128 * c : 128 * c + 128, :] = column_of(inverse * inverse * center)

    output = o_ref[...]
    scaled = g_s[...].astype(f32) * gain_ref[...]
    grad = (r_s[...] * (scaled - output * c_s[...]) / l_ref[...]).astype(bf16)
    wide = grad.astype(f32)
    row_dot = jnp.sum(wide * output, axis=1, keepdims=True)
    grad_t = jnp.transpose(wide).astype(bf16)
    query_t = jnp.transpose(q_s[...].astype(f32)).astype(bf16)
    past = (p1, p2, p3)

    def body(reach):
        spans = [(own, 0, 384, 0, 0, 256), (own, 0, 512, 0, 256, 256), (halo, 0, 128, OWN, 256, 256)]
        for d in range(reach):
            spans.append((past[d], 0, 512, OWN + HALO + 512 * d, 0, 512))
        grad_q = [None, None]
        for ref, k0, n, c0, r0, count in spans:
            e = e_ref[0, r0 : r0 + count, c0 : c0 + n]
            keys = ref[0:128, :] if ref is halo else ref[0, k0 : k0 + n, :]
            values = ref[128:256, :] if ref is halo else ref[1, k0 : k0 + n, :]
            grad_p = dot_nt(grad[r0 : r0 + count, :], values)
            grad_s = (e.astype(f32) * (grad_p - row_dot[r0 : r0 + count, :])).astype(bf16)
            t = dot_nn(grad_s, keys)
            for b in range(count // 256):
                i = r0 // 256 + b
                part = t[256 * b : 256 * b + 256]
                grad_q[i] = part if grad_q[i] is None else grad_q[i] + part
            dv_s[:, c0 : c0 + n] += dot_nn(grad_t[:, r0 : r0 + count], e)
            dk_s[:, c0 : c0 + n] += dot_nn(query_t[:, r0 : r0 + count], grad_s)
        dq_s[...] = (jnp.concatenate(grad_q, axis=0) * SCALE).astype(bf16)

    for reach in range(4):

        @pl.when(z == reach)
        def _():
            body(reach)

    for d, ref in enumerate((dq0, dq1, dq2, dq3)):
        ref[...] = dq_s[slot(x, d), :]

    @pl.when(head == GROUP - 1)
    def _():
        starts = (0, OWN, OWN + HALO, OWN + HALO + PAST, OWN + HALO + 2 * PAST)
        for ref, c0 in zip((d_own, d_halo, d_p1, d_p2, d_p3), starts):
            n = ref.shape[1]
            ref[0] = jnp.transpose(dk_s[:, c0 : c0 + n] * SCALE).astype(ref.dtype)
            ref[1] = jnp.transpose(dv_s[:, c0 : c0 + n]).astype(ref.dtype)


def backward(info, queries, cotangents, gain, sums, output, totals, weights, own, halo, past):
    key_part = jax.ShapeDtypeStruct((2, 512, 128), bf16)
    return pl.pallas_call(
        backward_kernel,
        name="attention_backward",
        grid_spec=pltpu.PrefetchScalarGridSpec(
            num_scalar_prefetch=1,
            grid=(GROUP,),
            in_specs=[per_head(128)] * 8
            + [per_head(1), all_of(8, 128), per_head(512), per_head(512)]
            + [pl.BlockSpec((1, 512, WIDTH), lambda g, i: (g, 0, 0))]
            + [all_of(2, 512, 128), all_of(272, 128)]
            + [all_of(2, 512, 128)] * 3,
            out_specs=[per_head(128)] * 4
            + [all_of(2, 512, 128), all_of(2, 128, 128)]
            + [all_of(2, 512, 128)] * 3,
            scratch_shapes=[pltpu.VMEM((512, 128), bf16)] * 3
            + [pltpu.VMEM((128, WIDTH), f32)] * 2
            + [pltpu.VMEM((512, 128), f32)] * 2,
        ),
        out_shape=[jax.ShapeDtypeStruct((128, GROUP * HD), bf16)] * 4
        + [jax.ShapeDtypeStruct((2, 512, 128), f32), jax.ShapeDtypeStruct((2, 128, 128), bf16)]
        + [key_part] * 3,
    )(info, *queries, *cotangents, gain, sums, output, totals, weights, own, halo, *past)


def along(x, axis, pairs):
    return lax.ppermute(x, axis, pairs)


def to_units(block, x):
    parts = []
    for d in range(4):
        unit = (x + d) & 3
        part = lax.dynamic_slice(
            block, (unit // 2, 0, (unit % 2) * GROUP * HD), (1, 128, GROUP * HD)
        )[0]
        parts.append(part if d == 0 else along(part, "ctx_1", [(i, (i + d) % 4) for i in range(4)]))
    return parts


def from_units(parts, x):
    got = [parts[0]]
    for d in range(1, 4):
        got.append(along(parts[d], "ctx_1", [(i, (i - d) % 4) for i in range(4)]))
    units = jnp.stack(got)
    units = jnp.stack([lax.dynamic_index_in_dim(units, (u - x) & 3, 0, False) for u in range(4)])
    units = units.reshape(2, 2, 128, GROUP * HD)
    return jnp.concatenate([units[:, 0], units[:, 1]], axis=-1)


def section_route(d, sign):
    route = []
    for s in range(4):
        for i in range(4):
            if sign > 0:
                unit = (i + d) % 4
                route.append((s * 4 + i, (s + unit // 2) % 4 * 4 + unit))
            else:
                route.append((s * 4 + i, (s - i // 2) % 4 * 4 + (i - d) % 4))
    return route


def on_device(query_heads, keys_values, grad_output, norm_gain, turn_ids):
    z = lax.axis_index("ctx_0")
    x = lax.axis_index("ctx_1")
    info = jnp.stack([x, z]).astype(jnp.int32)

    turn_rows = jnp.broadcast_to(turn_ids.astype(bf16)[None], (16, 128))
    kv = keys_values[0]
    heads = [
        jnp.concatenate([kv[:, 0, a : a + HD], kv[:, 1, a : a + HD], turn_rows], axis=0)
        for a in (0, HD)
    ]
    odd = (x & 1) == 1
    same = jnp.where(odd, heads[1], heads[0])
    other = jnp.where(odd, heads[0], heads[1])
    received = [
        along(same if d % 2 == 0 else other, ("section", "ctx_1"), section_route(d, 1))
        for d in range(4)
    ]
    queries = to_units(query_heads[0], x)
    own, first, turns = put_in_order(info, received)
    halo = along(first, "ctx_0", [(1, 0), (2, 1), (3, 2)])
    past1 = along(own, "ctx_0", [(0, 1), (1, 2), (2, 3)])
    past2 = along(own, "ctx_0", [(0, 2), (1, 3)])
    past3 = along(past2, "ctx_0", [(2, 3)])
    past = (past1, past2, past3)
    cotangents = to_units(grad_output[0], x)
    gain = lax.dynamic_slice(norm_gain[0], (x // 2, (x % 2) * GROUP * HD), (1, GROUP * HD))

    output, totals, weights = forward(info, queries, turns, own, halo, past)
    sums = token_sums(info, output, cotangents, gain)
    sums = sums + along(sums, "tp", [(i, i ^ 1) for i in range(4)])
    sums = sums + along(sums, "ctx_1", [(i, i ^ 1) for i in range(4)])
    sums = sums + along(sums, "tp", [(i, i ^ 2) for i in range(4)])
    normed = from_units(normed_parts(info, output, sums, gain), x)

    results = backward(
        info, queries, cotangents, gain, sums, output, totals, weights, own, halo, past
    )
    grad_q = from_units(results[:4], x)
    d_own, d_halo, d_p1, d_p2, d_p3 = results[4:]
    back1 = along(d_p1, "ctx_0", [(1, 0), (2, 1), (3, 2)])
    back2 = along(d_p2, "ctx_0", [(2, 0), (3, 1)])
    back3 = along(d_p3, "ctx_0", [(3, 0)])
    front = along(d_halo, "ctx_0", [(0, 1), (1, 2), (2, 3)])
    total = d_own + back1.astype(f32) + back2.astype(f32) + back3.astype(f32)
    total = total + jnp.pad(front.astype(f32), ((0, 0), (0, 384), (0, 0)))
    total = total.astype(bf16).reshape(2, 4, 128, HD)
    returned = []
    for d in range(4):
        part = lax.dynamic_index_in_dim(total, (x - d) & 3, 1, False)
        returned.append(along(part, ("section", "ctx_1"), section_route(d, -1)))
    alike = returned[0].astype(f32) + returned[2].astype(f32)
    differ = returned[1].astype(f32) + returned[3].astype(f32)
    low = jnp.where(odd, differ, alike)
    high = jnp.where(odd, alike, differ)
    kv_grad = jnp.concatenate([low, high], axis=-1).transpose(1, 0, 2)
    return normed[None], grad_q[None], kv_grad[None]


def solution(mesh):
    split = Mesh(
        mesh.devices.reshape(mesh.shape["section"], 4, 4, mesh.shape["tp"]),
        ("section", "ctx_0", "ctx_1", "tp"),
    )
    return jax.shard_map(
        on_device,
        mesh=split,
        in_specs=(
            P("section", None, CTX, "tp"),
            P("section", CTX, None, "tp"),
            P("section", None, CTX, "tp"),
            P("section", None, "tp"),
            P(CTX),
        ),
        out_specs=(
            P("section", None, CTX, "tp"),
            P("section", None, CTX, "tp"),
            P("section", CTX, None, "tp"),
        ),
        check_vma=False,
    )
```

time: 403 us -> 145 us (0.36)
  waiting for transfers between devices: 182 us -> 35.9 us
  local copies, waits for them, and re-layouts: 89.6 us -> 5.98 us
  matrix products: 38.8 us -> 0 us
  Pallas kernels: 0 us -> 31.7 us
  starting transfers between devices: 40 us -> 63.3 us
  other arithmetic: 24.4 us -> 5.9 us
  between operations: 14.4 us -> 1.24 us
  loops' own time: 11.6 us -> 0 us
    all_to_all x5 -> x0, waiting for transfers between devices: 90.9 us -> none  [sent_to_all(): lax.all_to_all(jnp.broadcast_to(x[None], (size, *x.shape)), axis, 0, 0, t...]
    reduce_scatter x2 -> x0, waiting for transfers between devices: 83.9 us -> none  [reduced_to_own(): parts = lax.psum_scatter(parts, axes[k], scatter_dimension=0, tiled=True)]
    ppermute x2 -> x31, starting transfers between devices: 4.66 us -> 63.3 us  [along(): return lax.ppermute(x, axis, pairs)]
    dot_general x56 -> x0, matrix products: 38.8 us -> none  [the longest x16 13.1 us: block_terms(): jnp.einsum('qhgd,khd->hgqk', queries, key_rows, preferred_element_type=jn...]
    all_to_all x5 -> x0, starting transfers between devices: 35.1 us -> none  [sent_to_all(): lax.all_to_all(jnp.broadcast_to(x[None], (size, *x.shape)), axis, 0, 0, t...]
    pallas_call x0 -> x5, Pallas kernels: none -> 31.7 us  [the longest x1 14.2 us: backward(): pl.pallas_call(backward_kernel, name='attention_backward', grid_spec=pltp...]
    ppermute x2 -> x31, waiting for transfers between devices: 7.55 us -> 35.9 us  [along(): return lax.ppermute(x, axis, pairs)]
    slice x19 -> x0, local copies, waits for them, and re-layouts: 15.9 us -> none  [the longest x16 13.1 us: block_terms(): value_rows = kv_rows[:, 1].reshape(row_count, head_count, HD)]
  transfers between devices with their start and end apart: 9 -> 31, of which waited for: 7 -> 11; matrix products, arithmetic and copies ran while one was open for 17% -> 4% of each run, Pallas kernels for 0% -> 17%
where the time goes in v1:
time: 145 us; the launch traced here: 144 us
  starting transfers between devices  63.3 us (44%)
  waiting for transfers between devices  35.9 us (25%)
  Pallas kernels  31.7 us (22%)
  local copies, waits for them, and re-layouts  5.98 us (4%)
  other arithmetic  5.9 us (4%)
    ppermute x31, starting transfers between devices, along(): return lax.ppermute(x, axis, pairs)  63.3 us
    ppermute x31, waiting for transfers between devices, along(): return lax.ppermute(x, axis, pairs)  35.9 us
    pallas_call x1, Pallas kernels, backward(): pl.pallas_call(backward_kernel, name='attention_backward', grid_spec=pltp...  14.2 us
    pallas_call x1, Pallas kernels, forward(): pl.pallas_call(forward_kernel, name='attention_forward', grid_spec=pltpu....  10.6 us
    unnamed x47, local copies, waits for them, and re-layouts  3.24 us
  transfers between devices with their start and end apart: 31, of which 11 were waited for; matrix products, arithmetic and copies ran while one was open for 4% of the time, Pallas kernels for 17%

profile of v1, /device:TPU:4, one launch (start us, length us, event | category | flops | bytes accessed | tf_op | source)
XLA Modules:
  0.0 144.0 jit_solution(3861454783553044348)
XLA Ops:
  2.4 3.5 %collective-permute-start.3 = (bf16[272,128]{1,0:T(8,128)(2,1)S(1)}, bf16[272,128]{1,0:T(8,128)(2,1)S(1)}, u32[]{:S(2)}, u32[]{:S(2)}) collective-permute-start(bf16[272,128]{1,0:T(8,128)(2,1)S(1)} %get-tuple-element.68), channel_id=1, source_target_pairs={{0,0},{4,4},{8,72},{12,76},{64,64},{68,68},{72,136},{76,140},{128,... | collective-permute-start | bytes 208904 | tf_op jit(solution)/shard_map/ppermute | solution.py:326
  6.0 2.3 %collective-permute-start.4 = (bf16[272,128]{1,0:T(8,128)(2,1)S(1)}, bf16[272,128]{1,0:T(8,128)(2,1)S(1)}, u32[]{:S(2)}, u32[]{:S(2)}) collective-permute-start(bf16[272,128]{1,0:T(8,128)(2,1)S(1)} %get-tuple-element.67), channel_id=1, source_target_pairs={{0,4},{4,72},{8,76},{12,0},{64,68},{68,136},{72,140},{76,64},{128,... | collective-permute-start | bytes 208904 | tf_op jit(solution)/shard_map/ppermute | solution.py:326
  8.3 1.4 collective-permute-start.6
  10.3 3.7 %collective-permute-done.4.a1 = bf16[272,128]{1,0:T(8,128)(2,1)S(1)} collective-permute-done((bf16[272,128]{1,0:T(8,128)(2,1)S(1)}, bf16[272,128]{1,0:T(8,128)(2,1)S(1)}, u32[]{:S(2)}, u32[]{:S(2)}) %collective-permute-start.4) | collective-permute-done | bytes 69664 | tf_op jit(solution)/shard_map/ppermute | solution.py:326
  16.1 1.8 %order_keys.1 = (bf16[2,512,128]{2,1,0:T(8,128)(2,1)}, bf16[272,128]{1,0:T(8,128)(2,1)}, f32[8,128]{1,0:T(8,128)}) custom-call(s32[2]{0:T(128)} %pad_add_fusion.info, bf16[272,128]{1,0:T(8,128)(2,1)} %copy-done.17, bf16[272,128]{1,0:T(8,128)(2,1)} %copy-done.19, bf16[272,128]{1,0:T(8,128)(2,1)} %copy-done.18, bf16[272,128]{1,0:T(8,128)(2,1)} %copy-done.20), custom_call_target="tpu_custom_call" | custom-call | tf_op jit(solution)/shard_map/order_keys/pallas_call | solution.py:59
  17.9 5.3 %collective-permute-start.9 = (bf16[2,512,128]{2,1,0:T(8,128)(2,1)}, bf16[2,512,128]{2,1,0:T(8,128)(2,1)S(1)}, u32[]{:S(2)}, u32[]{:S(2)}) collective-permute-start(bf16[2,512,128]{2,1,0:T(8,128)(2,1)} %get-tuple-element.23.own), channel_id=1, source_target_pairs={{0,32},{16,48},{1,33},{17,49},{2,34},{18,50},{3,35},{19,51},{4,36}... | collective-permute-start | bytes 786440 | tf_op jit(solution)/shard_map/ppermute | solution.py:326
  25.4 3.9 %collective-permute-start = (bf16[128,768]{1,0:T(8,128)(2,1)S(1)}, bf16[128,768]{1,0:T(8,128)(2,1)S(1)}, u32[]{:S(2)}, u32[]{:S(2)}) collective-permute-start(bf16[128,768]{1,0:T(8,128)(2,1)S(1)} %get-tuple-element.58), channel_id=1, source_target_pairs={{0,4},{4,8},{8,12},{12,0},{1,5},{5,9},{9,13},{13,1},{2,6},{6,10},{... | collective-permute-start | bytes 589832 | tf_op jit(solution)/shard_map/ppermute | solution.py:326
  29.3 1.5 %collective-permute-start.2 = (bf16[128,768]{1,0:T(8,128)(2,1)S(1)}, bf16[128,768]{1,0:T(8,128)(2,1)S(1)}, u32[]{:S(2)}, u32[]{:S(2)}) collective-permute-start(bf16[128,768]{1,0:T(8,128)(2,1)S(1)} %get-tuple-element.57), channel_id=1, source_target_pairs={{0,12},{4,0},{8,4},{12,8},{1,13},{5,1},{9,5},{13,9},{2,14},{6,2},{... | collective-permute-start | bytes 589832 | tf_op jit(solution)/shard_map/ppermute | solution.py:326
  30.7 4.6 %collective-permute-start.8 = (bf16[2,512,128]{2,1,0:T(8,128)(2,1)S(1)}, bf16[2,512,128]{2,1,0:T(8,128)(2,1)S(1)}, u32[]{:S(2)}, u32[]{:S(2)}) collective-permute-start(bf16[2,512,128]{2,1,0:T(8,128)(2,1)S(1)} %copy-done.1), channel_id=1, source_target_pairs={{0,16},{16,32},{32,48},{1,17},{17,33},{33,49},{2,18},{18,34},{34,5... | collective-permute-start | bytes 786440 | tf_op jit(solution)/shard_map/ppermute | solution.py:326
  36.8 2.1 %collective-permute-start.11 = (bf16[128,768]{1,0:T(8,128)(2,1)S(1)}, bf16[128,768]{1,0:T(8,128)(2,1)S(1)}, u32[]{:S(2)}, u32[]{:S(2)}) collective-permute-start(bf16[128,768]{1,0:T(8,128)(2,1)S(1)} %get-tuple-element.54), channel_id=1, source_target_pairs={{0,4},{4,8},{8,12},{12,0},{1,5},{5,9},{9,13},{13,1},{2,6},{6,10},{... | collective-permute-start | bytes 589832 | tf_op jit(solution)/shard_map/ppermute | solution.py:326
  38.9 1.9 %collective-permute-start.12 = (bf16[128,768]{1,0:T(8,128)(2,1)S(1)}, bf16[128,768]{1,0:T(8,128)(2,1)S(1)}, u32[]{:S(2)}, u32[]{:S(2)}) collective-permute-start(bf16[128,768]{1,0:T(8,128)(2,1)S(1)} %get-tuple-element.56), channel_id=1, source_target_pairs={{0,8},{4,12},{8,0},{12,4},{1,9},{5,13},{9,1},{13,5},{2,10},{6,14},... | collective-permute-start | bytes 589832 | tf_op jit(solution)/shard_map/ppermute | solution.py:326
  43.0 10.6 %attention_forward.1 = (f32[512,768]{1,0:T(8,128)}, f32[512,768]{1,0:T(8,128)}, bf16[6,512,2176]{2,1,0:T(8,128)(2,1)}) custom-call(s32[2]{0:T(128)} %pad_add_fusion.info, bf16[128,768]{1,0:T(8,128)(2,1)} %get-tuple-element.59.q0, bf16[128,768]{1,0:T(8,128)(2,1)} %copy-done.5, bf16[128,768]{1,0:T(8,128)(2,1)} %copy-done.6, bf16[128,768]{1,0:T(8,128)(2,1)} %copy-done.7, ...), custom_call_target="tpu_custom_call" | custom-call | tf_op jit(solution)/shard_map/attention_forward/pallas_call | solution.py:153
  54.4 2.7 %token_sums.1 = f32[8,128]{1,0:T(8,128)} custom-call(s32[2]{0:T(128)} %pad_add_fusion.info, f32[512,768]{1,0:T(8,128)} %get-tuple-element.25.o_ref, bf16[128,768]{1,0:T(8,128)(2,1)} %get-tuple-element.55.g0, bf16[128,768]{1,0:T(8,128)(2,1)} %copy-done.8, bf16[128,768]{1,0:T(8,128)(2,1)} %copy-done.9, bf16[128,768]{1,0:T(8,128)(2,1)} %copy-done.10, ...), custom_call_target="tpu_custom_call" | custom-call | tf_op jit(solution)/shard_map/token_sums/pallas_call | solution.py:199
  57.0 1.4 collective-permute-done.14
  59.1 1.4 collective-permute-start.15
  60.5 2.2 %collective-permute-done.15 = f32[8,128]{1,0:T(8,128)S(1)} collective-permute-done((f32[8,128]{1,0:T(8,128)S(1)}, f32[8,128]{1,0:T(8,128)S(1)}, u32[]{:S(2)}, u32[]{:S(2)}) %collective-permute-start.15) | collective-permute-done | bytes 4128 | tf_op jit(solution)/shard_map/ppermute | solution.py:326
  62.7 5.4 %collective-permute-start.16 = (f32[8,128]{1,0:T(8,128)S(1)}, f32[8,128]{1,0:T(8,128)S(1)}, u32[]{:S(2)}, u32[]{:S(2)}) collective-permute-start(f32[8,128]{1,0:T(8,128)S(1)} %add.156), channel_id=1, source_target_pairs={{0,2},{1,3},{2,0},{3,1},{4,6},{5,7},{6,4},{7,5},{8,10},{9,11},{10,... | collective-permute-start | bytes 12296 | tf_op jit(solution)/shard_map/ppermute | solution.py:326
  68.1 2.1 %collective-permute-done.16 = f32[8,128]{1,0:T(8,128)S(1)} collective-permute-done((f32[8,128]{1,0:T(8,128)S(1)}, f32[8,128]{1,0:T(8,128)S(1)}, u32[]{:S(2)}, u32[]{:S(2)}) %collective-permute-start.16) | collective-permute-done | bytes 4128 | tf_op jit(solution)/shard_map/ppermute | solution.py:326
  70.8 2.5 %normed_parts.1 = (bf16[128,768]{1,0:T(8,128)(2,1)}, bf16[128,768]{1,0:T(8,128)(2,1)}, bf16[128,768]{1,0:T(8,128)(2,1)}, bf16[128,768]{1,0:T(8,128)(2,1)}) custom-call(s32[2]{0:T(128)} %pad_add_fusion.info, f32[512,768]{1,0:T(8,128)} %get-tuple-element.25.o_ref, f32[8,128]{1,0:T(8,128)} %add.157.sums, f32[1,768]{1,0:T(1,128)} %fusion.gain_ref), custom_call_target="tpu_custom_call" | custom-call | tf_op jit(solution)/shard_map/normed_parts/pallas_call | solution.py:221
  73.3 1.5 %collective-permute-start.17 = (bf16[128,768]{1,0:T(8,128)(2,1)}, bf16[128,768]{1,0:T(8,128)(2,1)S(1)}, u32[]{:S(2)}, u32[]{:S(2)}) collective-permute-start(bf16[128,768]{1,0:T(8,128)(2,1)} %get-tuple-element.27), channel_id=1, source_target_pairs={{0,12},{4,0},{8,4},{12,8},{1,13},{5,1},{9,5},{13,9},{2,14},{6,2},{... | collective-permute-start | bytes 589832 | tf_op jit(solution)/shard_map/ppermute | solution.py:326
  74.8 1.9 %collective-permute-start.18 = (bf16[128,768]{1,0:T(8,128)(2,1)}, bf16[128,768]{1,0:T(8,128)(2,1)S(1)}, u32[]{:S(2)}, u32[]{:S(2)}) collective-permute-start(bf16[128,768]{1,0:T(8,128)(2,1)} %get-tuple-element.28), channel_id=1, source_target_pairs={{0,8},{4,12},{8,0},{12,4},{1,9},{5,13},{9,1},{13,5},{2,10},{6,14},... | collective-permute-start | bytes 589832 | tf_op jit(solution)/shard_map/ppermute | solution.py:326
  76.8 1.3 collective-permute-start.19
  78.1 14.2 %attention_backward.1 = (bf16[128,768]{1,0:T(8,128)(2,1)}, bf16[128,768]{1,0:T(8,128)(2,1)}, bf16[128,768]{1,0:T(8,128)(2,1)}, bf16[128,768]{1,0:T(8,128)(2,1)},...) custom-call(s32[2]{0:T(128)} %pad_add_fusion.info, ...), custom_call_target="tpu_custom_call" | custom-call | tf_op jit(solution)/shard_map/attention_backward/pallas_call | solution.py:301
  93.1 2.8 %collective-permute-start.21 = (bf16[128,768]{1,0:T(8,128)(2,1)}, bf16[128,768]{1,0:T(8,128)(2,1)S(1)}, u32[]{:S(2)}, u32[]{:S(2)}) collective-permute-start(bf16[128,768]{1,0:T(8,128)(2,1)} %get-tuple-element.34), channel_id=1, source_target_pairs={{0,8},{4,12},{8,0},{12,4},{1,9},{5,13},{9,1},{13,5},{2,10},{6,14},... | collective-permute-start | bytes 589832 | tf_op jit(solution)/shard_map/ppermute | solution.py:326
  97.2 1.3 collective-permute-start.24
  100.6 6.8 %collective-permute-start.26 = (bf16[2,128,128]{2,1,0:T(8,128)(2,1)S(1)}, bf16[2,128,128]{2,1,0:T(8,128)(2,1)S(1)}, u32[]{:S(2)}, u32[]{:S(2)}) collective-permute-start(bf16[2,128,128]{2,1,0:T(8,128)(2,1)S(1)} %copy-done.22), channel_id=1, source_target_pairs={{0,16},{16,32},{32,48},{1,17},{17,33},{33,49},{2,18},{18,34},{34,5... | collective-permute-start | bytes 196616 | tf_op jit(solution)/shard_map/ppermute | solution.py:326
  109.3 13.5 %collective-permute-done.24 = bf16[2,512,128]{2,1,0:T(8,128)(2,1)S(1)} collective-permute-done((bf16[2,512,128]{2,1,0:T(8,128)(2,1)}, bf16[2,512,128]{2,1,0:T(8,128)(2,1)S(1)}, u32[]{:S(2)}, u32[]{:S(2)}) %collective-permute-start.24) | collective-permute-done | bytes 262176 | tf_op jit(solution)/shard_map/ppermute | solution.py:326
  122.9 8.7 %collective-permute-done.25 = bf16[2,512,128]{2,1,0:T(8,128)(2,1)S(1)} collective-permute-done((bf16[2,512,128]{2,1,0:T(8,128)(2,1)S(1)}, bf16[2,512,128]{2,1,0:T(8,128)(2,1)S(1)}, u32[]{:S(2)}, u32[]{:S(2)}) %collective-permute-start.25) | collective-permute-done | bytes 262176 | tf_op jit(solution)/shard_map/ppermute | solution.py:326
  131.9 2.2 %collective-permute-start.28 = (bf16[2,128,128]{2,0,1:T(2,128)(2,1)S(1)}, bf16[2,128,128]{2,0,1:T(2,128)(2,1)S(1)}, u32[]{:S(2)}, u32[]{:S(2)}) collective-permute-start(bf16[2,128,128]{2,0,1:T(2,128)(2,1)S(1)} %bitcast.102), channel_id=1, source_target_pairs={{0,4},{4,8},{8,204},{12,192},{64,68},{68,72},{72,12},{76,0},{128,1... | collective-permute-start | bytes 196616 | tf_op jit(solution)/shard_map/ppermute | solution.py:326
  134.3 2.6 %collective-permute-start.30 = (bf16[2,128,128]{2,0,1:T(2,128)(2,1)S(1)}, bf16[2,128,128]{2,0,1:T(2,128)(2,1)S(1)}, u32[]{:S(2)}, u32[]{:S(2)}) collective-permute-start(bf16[2,128,128]{2,0,1:T(2,128)(2,1)S(1)} %bitcast.104), channel_id=1, source_target_pairs={{0,8},{4,12},{8,192},{12,196},{64,72},{68,76},{72,0},{76,4},{128,1... | collective-permute-start | bytes 196616 | tf_op jit(solution)/shard_map/ppermute | solution.py:326
  137.0 3.4 %collective-permute-start.29 = (bf16[2,128,128]{2,0,1:T(2,128)(2,1)S(1)}, bf16[2,128,128]{2,0,1:T(2,128)(2,1)S(1)}, u32[]{:S(2)}, u32[]{:S(2)}) collective-permute-start(bf16[2,128,128]{2,0,1:T(2,128)(2,1)S(1)} %bitcast.105), channel_id=1, source_target_pairs={{0,0},{4,4},{8,200},{12,204},{64,64},{68,68},{72,8},{76,12},{128,1... | collective-permute-start | bytes 196616 | tf_op jit(solution)/shard_map/ppermute | solution.py:326
  141.4 1.8 %collective-permute-done.29 = bf16[2,128,128]{2,0,1:T(2,128)(2,1)S(1)} collective-permute-done((bf16[2,128,128]{2,0,1:T(2,128)(2,1)S(1)}, bf16[2,128,128]{2,0,1:T(2,128)(2,1)S(1)}, u32[]{:S(2)}, u32[]{:S(2)}) %collective-permute-start.29) | collective-permute-done | bytes 65568 | tf_op jit(solution)/shard_map/ppermute | solution.py:326
  (110 shorter events, 20.5 us)
Async XLA Ops:
  0.6 40.9 %copy-start = (f32[1,2,1536]{2,1,0:T(2,128)S(1)}, f32[1,2,1536]{2,1,0:T(2,128)}, u32[]{:S(2)}) copy-start(f32[1,2,1536]{2,1,0:T(2,128)} %param.8) | copy-start | bytes 36868
  2.4 7.9 %collective-permute-start.3 = (bf16[272,128]{1,0:T(8,128)(2,1)S(1)}, bf16[272,128]{1,0:T(8,128)(2,1)S(1)}, u32[]{:S(2)}, u32[]{:S(2)}) collective-permute-start(bf16[272,128]{1,0:T(8,128)(2,1)S(1)} %get-tuple-element.68), channel_id=1, source_target_pairs={{0,0},{4,4},{8,72},{12,76},{64,64},{68,68},{72,136},{76,140},{128,... | collective-permute-start | bytes 208904 | tf_op jit(solution)/shard_map/ppermute | solution.py:326
  5.9 8.8 %collective-permute-start.5 = (bf16[272,128]{1,0:T(8,128)(2,1)S(1)}, bf16[272,128]{1,0:T(8,128)(2,1)S(1)}, u32[]{:S(2)}, u32[]{:S(2)}) collective-permute-start(bf16[272,128]{1,0:T(8,128)(2,1)S(1)} %get-tuple-element.68), channel_id=1, source_target_pairs={{0,72},{4,76},{8,0},{12,4},{64,136},{68,140},{72,64},{76,68},{128,... | collective-permute-start | bytes 208904 | tf_op jit(solution)/shard_map/ppermute | solution.py:326
  6.0 8.0 %collective-permute-start.4 = (bf16[272,128]{1,0:T(8,128)(2,1)S(1)}, bf16[272,128]{1,0:T(8,128)(2,1)S(1)}, u32[]{:S(2)}, u32[]{:S(2)}) collective-permute-start(bf16[272,128]{1,0:T(8,128)(2,1)S(1)} %get-tuple-element.67), channel_id=1, source_target_pairs={{0,4},{4,72},{8,76},{12,0},{64,68},{68,136},{72,140},{76,64},{128,... | collective-permute-start | bytes 208904 | tf_op jit(solution)/shard_map/ppermute | solution.py:326
  8.3 7.2 %collective-permute-start.6 = (bf16[272,128]{1,0:T(8,128)(2,1)S(1)}, bf16[272,128]{1,0:T(8,128)(2,1)S(1)}, u32[]{:S(2)}, u32[]{:S(2)}) collective-permute-start(bf16[272,128]{1,0:T(8,128)(2,1)S(1)} %get-tuple-element.67), channel_id=1, source_target_pairs={{0,76},{4,0},{8,4},{12,72},{64,140},{68,64},{72,68},{76,136},{128,... | collective-permute-start | bytes 208904 | tf_op jit(solution)/shard_map/ppermute | solution.py:326
  17.9 17.4 %collective-permute-start.9 = (bf16[2,512,128]{2,1,0:T(8,128)(2,1)}, bf16[2,512,128]{2,1,0:T(8,128)(2,1)S(1)}, u32[]{:S(2)}, u32[]{:S(2)}) collective-permute-start(bf16[2,512,128]{2,1,0:T(8,128)(2,1)} %get-tuple-element.23.own), channel_id=1, source_target_pairs={{0,32},{16,48},{1,33},{17,49},{2,34},{18,50},{3,35},{19,51},{4,36}... | collective-permute-start | bytes 786440 | tf_op jit(solution)/shard_map/ppermute | solution.py:326
  23.3 7.4 %collective-permute-start.7 = (bf16[272,128]{1,0:T(8,128)(2,1)}, bf16[272,128]{1,0:T(8,128)(2,1)S(1)}, u32[]{:S(2)}, u32[]{:S(2)}) collective-permute-start(bf16[272,128]{1,0:T(8,128)(2,1)} %get-tuple-element.24), channel_id=1, source_target_pairs={{16,0},{32,16},{48,32},{17,1},{33,17},{49,33},{18,2},{34,18},{50,3... | collective-permute-start | bytes 208904 | tf_op jit(solution)/shard_map/ppermute | solution.py:326
  25.4 11.4 %collective-permute-start = (bf16[128,768]{1,0:T(8,128)(2,1)S(1)}, bf16[128,768]{1,0:T(8,128)(2,1)S(1)}, u32[]{:S(2)}, u32[]{:S(2)}) collective-permute-start(bf16[128,768]{1,0:T(8,128)(2,1)S(1)} %get-tuple-element.58), channel_id=1, source_target_pairs={{0,4},{4,8},{8,12},{12,0},{1,5},{5,9},{9,13},{13,1},{2,6},{6,10},{... | collective-permute-start | bytes 589832 | tf_op jit(solution)/shard_map/ppermute | solution.py:326
  29.3 9.7 %collective-permute-start.1 = (bf16[128,768]{1,0:T(8,128)(2,1)S(1)}, bf16[128,768]{1,0:T(8,128)(2,1)S(1)}, u32[]{:S(2)}, u32[]{:S(2)}) collective-permute-start(bf16[128,768]{1,0:T(8,128)(2,1)S(1)} %get-tuple-element.60), channel_id=1, source_target_pairs={{0,8},{4,12},{8,0},{12,4},{1,9},{5,13},{9,1},{13,5},{2,10},{6,14},... | collective-permute-start | bytes 589832 | tf_op jit(solution)/shard_map/ppermute | solution.py:326
  29.3 11.6 %collective-permute-start.2 = (bf16[128,768]{1,0:T(8,128)(2,1)S(1)}, bf16[128,768]{1,0:T(8,128)(2,1)S(1)}, u32[]{:S(2)}, u32[]{:S(2)}) collective-permute-start(bf16[128,768]{1,0:T(8,128)(2,1)S(1)} %get-tuple-element.57), channel_id=1, source_target_pairs={{0,12},{4,0},{8,4},{12,8},{1,13},{5,1},{9,5},{13,9},{2,14},{6,2},{... | collective-permute-start | bytes 589832 | tf_op jit(solution)/shard_map/ppermute | solution.py:326
  30.7 11.4 %collective-permute-start.8 = (bf16[2,512,128]{2,1,0:T(8,128)(2,1)S(1)}, bf16[2,512,128]{2,1,0:T(8,128)(2,1)S(1)}, u32[]{:S(2)}, u32[]{:S(2)}) collective-permute-start(bf16[2,512,128]{2,1,0:T(8,128)(2,1)S(1)} %copy-done.1), channel_id=1, source_target_pairs={{0,16},{16,32},{32,48},{1,17},{17,33},{33,49},{2,18},{18,34},{34,5... | collective-permute-start | bytes 786440 | tf_op jit(solution)/shard_map/ppermute | solution.py:326
  35.3 6.9 %collective-permute-start.10 = (bf16[2,512,128]{2,1,0:T(8,128)(2,1)S(1)}, bf16[2,512,128]{2,1,0:T(8,128)(2,1)S(1)}, u32[]{:S(2)}, u32[]{:S(2)}) collective-permute-start(bf16[2,512,128]{2,1,0:T(8,128)(2,1)S(1)} %collective-permute-done.9.p2), channel_id=1, source_target_pairs={{32,48},{33,49},{34,50},{35,51},{36,52},{37,53},{38,54},{39,55},{4... | collective-permute-start | bytes 786440 | tf_op jit(solution)/shard_map/ppermute | solution.py:326
  36.8 16.8 %collective-permute-start.11 = (bf16[128,768]{1,0:T(8,128)(2,1)S(1)}, bf16[128,768]{1,0:T(8,128)(2,1)S(1)}, u32[]{:S(2)}, u32[]{:S(2)}) collective-permute-start(bf16[128,768]{1,0:T(8,128)(2,1)S(1)} %get-tuple-element.54), channel_id=1, source_target_pairs={{0,4},{4,8},{8,12},{12,0},{1,5},{5,9},{9,13},{13,1},{2,6},{6,10},{... | collective-permute-start | bytes 589832 | tf_op jit(solution)/shard_map/ppermute | solution.py:326
  38.9 14.6 %collective-permute-start.12 = (bf16[128,768]{1,0:T(8,128)(2,1)S(1)}, bf16[128,768]{1,0:T(8,128)(2,1)S(1)}, u32[]{:S(2)}, u32[]{:S(2)}) collective-permute-start(bf16[128,768]{1,0:T(8,128)(2,1)S(1)} %get-tuple-element.56), channel_id=1, source_target_pairs={{0,8},{4,12},{8,0},{12,4},{1,9},{5,13},{9,1},{13,5},{2,10},{6,14},... | collective-permute-start | bytes 589832 | tf_op jit(solution)/shard_map/ppermute | solution.py:326
  40.9 12.7 %collective-permute-start.13 = (bf16[128,768]{1,0:T(8,128)(2,1)S(1)}, bf16[128,768]{1,0:T(8,128)(2,1)S(1)}, u32[]{:S(2)}, u32[]{:S(2)}) collective-permute-start(bf16[128,768]{1,0:T(8,128)(2,1)S(1)} %get-tuple-element.53), channel_id=1, source_target_pairs={{0,12},{4,0},{8,4},{12,8},{1,13},{5,1},{9,5},{13,9},{2,14},{6,2},{... | collective-permute-start | bytes 589832 | tf_op jit(solution)/shard_map/ppermute | solution.py:326
  57.0 1.4 collective-permute-start.14
  59.1 3.6 %collective-permute-start.15 = (f32[8,128]{1,0:T(8,128)S(1)}, f32[8,128]{1,0:T(8,128)S(1)}, u32[]{:S(2)}, u32[]{:S(2)}) collective-permute-start(f32[8,128]{1,0:T(8,128)S(1)} %add.155), channel_id=1, source_target_pairs={{0,4},{4,0},{8,12},{12,8},{1,5},{5,1},{9,13},{13,9},{2,6},{6,2},{1... | collective-permute-start | bytes 12296 | tf_op jit(solution)/shard_map/ppermute | solution.py:326
  62.7 7.5 %collective-permute-start.16 = (f32[8,128]{1,0:T(8,128)S(1)}, f32[8,128]{1,0:T(8,128)S(1)}, u32[]{:S(2)}, u32[]{:S(2)}) collective-permute-start(f32[8,128]{1,0:T(8,128)S(1)} %add.156), channel_id=1, source_target_pairs={{0,2},{1,3},{2,0},{3,1},{4,6},{5,7},{6,4},{7,5},{8,10},{9,11},{10,... | collective-permute-start | bytes 12296 | tf_op jit(solution)/shard_map/ppermute | solution.py:326
  73.3 22.6 %collective-permute-start.17 = (bf16[128,768]{1,0:T(8,128)(2,1)}, bf16[128,768]{1,0:T(8,128)(2,1)S(1)}, u32[]{:S(2)}, u32[]{:S(2)}) collective-permute-start(bf16[128,768]{1,0:T(8,128)(2,1)} %get-tuple-element.27), channel_id=1, source_target_pairs={{0,12},{4,0},{8,4},{12,8},{1,13},{5,1},{9,5},{13,9},{2,14},{6,2},{... | collective-permute-start | bytes 589832 | tf_op jit(solution)/shard_map/ppermute | solution.py:326
  74.8 21.1 %collective-permute-start.18 = (bf16[128,768]{1,0:T(8,128)(2,1)}, bf16[128,768]{1,0:T(8,128)(2,1)S(1)}, u32[]{:S(2)}, u32[]{:S(2)}) collective-permute-start(bf16[128,768]{1,0:T(8,128)(2,1)} %get-tuple-element.28), channel_id=1, source_target_pairs={{0,8},{4,12},{8,0},{12,4},{1,9},{5,13},{9,1},{13,5},{2,10},{6,14},... | collective-permute-start | bytes 589832 | tf_op jit(solution)/shard_map/ppermute | solution.py:326
  76.8 20.4 %collective-permute-start.19 = (bf16[128,768]{1,0:T(8,128)(2,1)}, bf16[128,768]{1,0:T(8,128)(2,1)S(1)}, u32[]{:S(2)}, u32[]{:S(2)}) collective-permute-start(bf16[128,768]{1,0:T(8,128)(2,1)} %get-tuple-element.29), channel_id=1, source_target_pairs={{0,4},{4,8},{8,12},{12,0},{1,5},{5,9},{9,13},{13,1},{2,6},{6,10},{... | collective-permute-start | bytes 589832 | tf_op jit(solution)/shard_map/ppermute | solution.py:326
  92.3 6.3 %collective-permute-start.20 = (bf16[128,768]{1,0:T(8,128)(2,1)}, bf16[128,768]{1,0:T(8,128)(2,1)S(1)}, u32[]{:S(2)}, u32[]{:S(2)}) collective-permute-start(bf16[128,768]{1,0:T(8,128)(2,1)} %get-tuple-element.33), channel_id=1, source_target_pairs={{0,12},{4,0},{8,4},{12,8},{1,13},{5,1},{9,5},{13,9},{2,14},{6,2},{... | collective-permute-start | bytes 589832 | tf_op jit(solution)/shard_map/ppermute | solution.py:326
  93.1 7.5 %collective-permute-start.21 = (bf16[128,768]{1,0:T(8,128)(2,1)}, bf16[128,768]{1,0:T(8,128)(2,1)S(1)}, u32[]{:S(2)}, u32[]{:S(2)}) collective-permute-start(bf16[128,768]{1,0:T(8,128)(2,1)} %get-tuple-element.34), channel_id=1, source_target_pairs={{0,8},{4,12},{8,0},{12,4},{1,9},{5,13},{9,1},{13,5},{2,10},{6,14},... | collective-permute-start | bytes 589832 | tf_op jit(solution)/shard_map/ppermute | solution.py:326
  95.9 11.5 %collective-permute-start.22 = (bf16[128,768]{1,0:T(8,128)(2,1)}, bf16[128,768]{1,0:T(8,128)(2,1)S(1)}, u32[]{:S(2)}, u32[]{:S(2)}) collective-permute-start(bf16[128,768]{1,0:T(8,128)(2,1)} %get-tuple-element.35), channel_id=1, source_target_pairs={{0,4},{4,8},{8,12},{12,0},{1,5},{5,9},{9,13},{13,1},{2,6},{6,10},{... | collective-permute-start | bytes 589832 | tf_op jit(solution)/shard_map/ppermute | solution.py:326
  95.9 13.4 %collective-permute-start.23 = (bf16[2,512,128]{2,1,0:T(8,128)(2,1)}, bf16[2,512,128]{2,1,0:T(8,128)(2,1)S(1)}, u32[]{:S(2)}, u32[]{:S(2)}) collective-permute-start(bf16[2,512,128]{2,1,0:T(8,128)(2,1)} %get-tuple-element.37), channel_id=1, source_target_pairs={{16,0},{32,16},{48,32},{17,1},{33,17},{49,33},{18,2},{34,18},{50,3... | collective-permute-start | bytes 786440 | tf_op jit(solution)/shard_map/ppermute | solution.py:326
  97.2 25.6 %collective-permute-start.24 = (bf16[2,512,128]{2,1,0:T(8,128)(2,1)}, bf16[2,512,128]{2,1,0:T(8,128)(2,1)S(1)}, u32[]{:S(2)}, u32[]{:S(2)}) collective-permute-start(bf16[2,512,128]{2,1,0:T(8,128)(2,1)} %get-tuple-element.38), channel_id=1, source_target_pairs={{32,0},{48,16},{33,1},{49,17},{34,2},{50,18},{35,3},{51,19},{36,4}... | collective-permute-start | bytes 786440 | tf_op jit(solution)/shard_map/ppermute | solution.py:326
  98.7 32.9 %collective-permute-start.25 = (bf16[2,512,128]{2,1,0:T(8,128)(2,1)S(1)}, bf16[2,512,128]{2,1,0:T(8,128)(2,1)S(1)}, u32[]{:S(2)}, u32[]{:S(2)}) collective-permute-start(bf16[2,512,128]{2,1,0:T(8,128)(2,1)S(1)} %copy-done.21), channel_id=1, source_target_pairs={{48,0},{49,1},{50,2},{51,3},{52,4},{53,5},{54,6},{55,7},{56,8},{57... | collective-permute-start | bytes 786440 | tf_op jit(solution)/shard_map/ppermute | solution.py:326
  100.6 8.7 %collective-permute-start.26 = (bf16[2,128,128]{2,1,0:T(8,128)(2,1)S(1)}, bf16[2,128,128]{2,1,0:T(8,128)(2,1)S(1)}, u32[]{:S(2)}, u32[]{:S(2)}) collective-permute-start(bf16[2,128,128]{2,1,0:T(8,128)(2,1)S(1)} %copy-done.22), channel_id=1, source_target_pairs={{0,16},{16,32},{32,48},{1,17},{17,33},{33,49},{2,18},{18,34},{34,5... | collective-permute-start | bytes 196616 | tf_op jit(solution)/shard_map/ppermute | solution.py:326
  131.9 9.5 %collective-permute-start.28 = (bf16[2,128,128]{2,0,1:T(2,128)(2,1)S(1)}, bf16[2,128,128]{2,0,1:T(2,128)(2,1)S(1)}, u32[]{:S(2)}, u32[]{:S(2)}) collective-permute-start(bf16[2,128,128]{2,0,1:T(2,128)(2,1)S(1)} %bitcast.102), channel_id=1, source_target_pairs={{0,4},{4,8},{8,204},{12,192},{64,68},{68,72},{72,12},{76,0},{128,1... | collective-permute-start | bytes 196616 | tf_op jit(solution)/shard_map/ppermute | solution.py:326
  134.2 7.2 %collective-permute-start.27 = (bf16[2,128,128]{2,0,1:T(2,128)(2,1)S(1)}, bf16[2,128,128]{2,0,1:T(2,128)(2,1)S(1)}, u32[]{:S(2)}, u32[]{:S(2)}) collective-permute-start(bf16[2,128,128]{2,0,1:T(2,128)(2,1)S(1)} %bitcast.103), channel_id=1, source_target_pairs={{0,12},{4,0},{8,196},{12,200},{64,76},{68,64},{72,4},{76,8},{128,1... | collective-permute-start | bytes 196616 | tf_op jit(solution)/shard_map/ppermute | solution.py:326
  134.3 7.0 %collective-permute-start.30 = (bf16[2,128,128]{2,0,1:T(2,128)(2,1)S(1)}, bf16[2,128,128]{2,0,1:T(2,128)(2,1)S(1)}, u32[]{:S(2)}, u32[]{:S(2)}) collective-permute-start(bf16[2,128,128]{2,0,1:T(2,128)(2,1)S(1)} %bitcast.104), channel_id=1, source_target_pairs={{0,8},{4,12},{8,192},{12,196},{64,72},{68,76},{72,0},{76,4},{128,1... | collective-permute-start | bytes 196616 | tf_op jit(solution)/shard_map/ppermute | solution.py:326
  137.0 6.2 %collective-permute-start.29 = (bf16[2,128,128]{2,0,1:T(2,128)(2,1)S(1)}, bf16[2,128,128]{2,0,1:T(2,128)(2,1)S(1)}, u32[]{:S(2)}, u32[]{:S(2)}) collective-permute-start(bf16[2,128,128]{2,0,1:T(2,128)(2,1)S(1)} %bitcast.105), channel_id=1, source_target_pairs={{0,0},{4,4},{8,200},{12,204},{64,64},{68,68},{72,8},{76,12},{128,1... | collective-permute-start | bytes 196616 | tf_op jit(solution)/shard_map/ppermute | solution.py:326
  (22 other events, 186.2 us)

commit v2 on v1

v2 whole, which is shorter than its diff:
```python
import math

import jax
import jax.numpy as jnp
from jax import lax
from jax.experimental import pallas as pl
from jax.experimental.pallas import tpu as pltpu
from jax.sharding import Mesh
from jax.sharding import PartitionSpec as P


HD = 128
KVH = 8
GROUP = 6
FEATURES = KVH * GROUP * HD
CTX = ("ctx_0", "ctx_1")
OWN, HALO, PAST = 512, 128, 512
NEAR, FAR = OWN + HALO + PAST, 2 * PAST
SCALE = HD**-0.5
SCALE_LOG2 = SCALE * math.log2(math.e)


neg_big = -1e30
eps_norm = 1e-06
bf16 = jnp.bfloat16
f32 = jnp.float32


def dot_nt(a, b):
    return lax.dot_general(a, b, (((1,), (1,)), ((), ())), preferred_element_type=f32)


def dot_nn(a, b):
    return lax.dot_general(a, b, (((1,), (0,)), ((), ())), preferred_element_type=f32)


def slot(x, d):
    return pl.ds(pl.multiple_of(((x - d) & 3) * 128, 128), 128)


def column_of(row):
    return jnp.transpose(jnp.broadcast_to(row, (128, 128)))


def order_kernel(info, a0, a1, a2, a3, own, first, turns):
    x = info[0]
    for d, ref in enumerate((a0, a1, a2, a3)):
        rows = slot(x, d)
        own[0, rows, :] = ref[0:128, :]
        own[1, rows, :] = ref[128:256, :]
        at = (x - d) & 3
        turns[pl.ds(at, 1), :] = ref[256:272, :].astype(f32)[0:1, :]

        @pl.when(at == 0)
        def _():
            first[...] = ref[...]


def put_in_order(info, parts):
    whole = pl.BlockSpec(memory_space=pltpu.VMEM)
    return pl.pallas_call(
        order_kernel,
        name="order_keys",
        in_specs=[pl.BlockSpec(memory_space=pltpu.SMEM)] + [whole] * 4,
        out_specs=[whole] * 3,
        out_shape=[
            jax.ShapeDtypeStruct((2, 512, 128), bf16),
            jax.ShapeDtypeStruct((272, 128), bf16),
            jax.ShapeDtypeStruct((8, 128), f32),
        ],
    )(info, *parts)


KEPT = pl.BlockSpec(memory_space=pltpu.VMEM)
LIMIT = pltpu.CompilerParams(vmem_limit_bytes=28 << 20)


def per_head(rows, at=0):
    return pl.BlockSpec((rows, 128), lambda g, i: (at, g))


def all_of(*shape):
    return pl.BlockSpec(shape, lambda g, i: (0,) * len(shape))


def keys_of(ref, k0, n):
    return ref[k0 : k0 + n, :] if len(ref.shape) == 2 else ref[0, k0 : k0 + n, :]


def values_of(ref, k0, n):
    return ref[128 + k0 : 128 + k0 + n, :] if len(ref.shape) == 2 else ref[1, k0 : k0 + n, :]


def forward_kernel(
    info, q0, q1, q2, q3, g0, g1, g2, g3, gain_ref, turns, own, halo, p1, p2, p3,
    o_ref, l_ref, near_ref, far_ref, sums_ref, q_s, g_s, s_s, t_s, sq_s, dot_s,
):
    x, z = info[0], info[1]
    head = pl.program_id(0)
    for d, (a, b) in enumerate(((q0, g0), (q1, g1), (q2, g2), (q3, g3))):
        q_s[slot(x, d), :] = a[...]
        g_s[slot(x, d), :] = b[...]

    @pl.when(head == 0)
    def _():
        sq_s[...] = jnp.zeros_like(sq_s)
        dot_s[...] = jnp.zeros_like(dot_s)
        for c in range(4):
            t_s[128 * c : 128 * c + 128, :] = column_of(turns[c : c + 1, :])

    halo_turns = halo[256:272, :].astype(f32)[0:1, :]

    def masked(s, b, first_key, count):
        tiles = []
        row = 256 * b + lax.broadcasted_iota(jnp.int32, (256, 128), 0)
        lane = lax.broadcasted_iota(jnp.int32, (256, 128), 1)
        mine = t_s[256 * b : 256 * b + 256, :]
        for j in range(count // 128):
            c = first_key // 128 + j
            theirs = turns[c : c + 1, :] if c < 4 else halo_turns
            seen = (lane + 128 * c <= row) | (mine == theirs)
            tiles.append(jnp.where(seen, s[:, 128 * j : 128 * j + 128], neg_big))
        return jnp.concatenate(tiles, axis=1)

    def block(b, reach):
        rows = pl.ds(256 * b, 256)
        q = q_s[rows, :]
        if b == 0:
            spans = [(own, 0, 384, near_ref, 0, True)]
        else:
            spans = [
                (own, 0, 256, near_ref, 0, False),
                (own, 256, 256, near_ref, 256, True),
                (halo, 0, 128, near_ref, OWN, True),
            ]
        if reach > 0:
            spans.append((p1, 0, 512, near_ref, OWN + HALO, False))
        if reach > 1:
            spans.append((p2, 0, 512, far_ref, 0, False))
        if reach > 2:
            spans.append((p3, 0, 512, far_ref, PAST, False))
        top = None
        for ref, k0, n, to, c0, partial in spans:
            s = dot_nt(q, keys_of(ref, k0, n))
            if partial:
                s = masked(s, b, c0, n)
            at = c0 + (NEAR if to is far_ref else 0)
            s_s[rows, at : at + n] = s
            for j in range(n // 128):
                t = s[:, 128 * j : 128 * j + 128]
                top = t if top is None else jnp.maximum(top, t)
        top = jnp.max(top, axis=1, keepdims=True) * SCALE_LOG2
        total = mixed = None
        for ref, k0, n, to, c0, _ in spans:
            at = c0 + (NEAR if to is far_ref else 0)
            e = jnp.exp2(s_s[rows, at : at + n] * SCALE_LOG2 - top)
            for j in range(n // 128):
                t = e[:, 128 * j : 128 * j + 128]
                total = t if total is None else total + t
            e = e.astype(bf16)
            to[head, rows, c0 : c0 + n] = e
            t = dot_nn(e, values_of(ref, k0, n))
            mixed = t if mixed is None else mixed + t
        total = jnp.sum(total, axis=1, keepdims=True)
        o = mixed / total
        o_ref[head, rows, :] = o
        l_ref[head, rows, :] = jnp.broadcast_to(total, (256, 128))
        sq_s[rows, :] += o * o
        dot_s[rows, :] += g_s[rows, :].astype(f32) * gain_ref[...] * o

    for reach in range(4):

        @pl.when(z == reach)
        def _():
            block(0, reach)
            block(1, reach)

    @pl.when(head == GROUP - 1)
    def _():
        for c in range(4):
            rows = pl.ds(128 * c, 128)
            sums_ref[c : c + 1, :] = jnp.sum(jnp.transpose(sq_s[rows, :]), axis=0, keepdims=True)
            sums_ref[4 + c : 5 + c, :] = jnp.sum(
                jnp.transpose(dot_s[rows, :]), axis=0, keepdims=True
            )


def forward(info, parts, gain, turns, own, halo, past):
    return pl.pallas_call(
        forward_kernel,
        name="attention_forward",
        grid_spec=pltpu.PrefetchScalarGridSpec(
            num_scalar_prefetch=1,
            grid=(GROUP,),
            in_specs=[per_head(128)] * 4
            + [per_head(128, 1)] * 4
            + [per_head(1), all_of(8, 128), all_of(2, 512, 128), all_of(272, 128)]
            + [all_of(2, 512, 128)] * 3,
            out_specs=[KEPT] * 4 + [all_of(8, 128)],
            scratch_shapes=[
                pltpu.VMEM((512, 128), bf16),
                pltpu.VMEM((512, 128), bf16),
                pltpu.VMEM((512, NEAR + FAR), f32),
                pltpu.VMEM((512, 128), f32),
                pltpu.VMEM((512, 128), f32),
                pltpu.VMEM((512, 128), f32),
            ],
        ),
        out_shape=[
            pltpu.VMEM((GROUP, 512, HD), f32),
            pltpu.VMEM((GROUP, 512, HD), f32),
            pltpu.VMEM((GROUP, 512, NEAR), bf16),
            pltpu.VMEM((GROUP, 512, FAR), bf16),
            jax.ShapeDtypeStruct((8, 128), f32),
        ],
        compiler_params=LIMIT,
    )(info, *parts, *parts, gain, turns, own, halo, *past)


def cotangent_rows(q_s, g_s, gain_ref, r_s, c_s, o_ref, l_ref):
    output = o_ref[pl.program_id(0)]
    scaled = g_s[...].astype(f32) * gain_ref[...]
    grad = (r_s[...] * (scaled - output * c_s[...]) / l_ref[pl.program_id(0)]).astype(bf16)
    wide = grad.astype(f32)
    row_dot = jnp.sum(wide * output, axis=1, keepdims=True)
    grad_t = jnp.transpose(wide).astype(bf16)
    query_t = jnp.transpose(q_s[...].astype(f32)).astype(bf16)
    return grad, row_dot, grad_t, query_t


def fill_columns(sums, r_s, c_s):
    for c in range(4):
        inverse = lax.rsqrt(sums[c : c + 1, :] / FEATURES + eps_norm)
        center = sums[4 + c : 5 + c, :] / FEATURES
        r_s[128 * c : 128 * c + 128, :] = column_of(inverse)
        c_s[128 * c : 128 * c + 128, :] = column_of(inverse * inverse * center)


def spans_back(spans, e_ref, rows_of, grad_q, dk_s, dv_s):
    grad, row_dot, grad_t, query_t = rows_of
    for ref, k0, n, c0, r0, count in spans:
        e = e_ref[pl.program_id(0), r0 : r0 + count, c0 : c0 + n]
        grad_p = dot_nt(grad[r0 : r0 + count, :], values_of(ref, k0, n))
        grad_s = (e.astype(f32) * (grad_p - row_dot[r0 : r0 + count, :])).astype(bf16)
        t = dot_nn(grad_s, keys_of(ref, k0, n))
        for b in range(count // 256):
            i = r0 // 256 + b
            part = t[256 * b : 256 * b + 256]
            grad_q[i] = part if grad_q[i] is None else grad_q[i] + part
        dv_s[:, c0 : c0 + n] += dot_nn(grad_t[:, r0 : r0 + count], e)
        dk_s[:, c0 : c0 + n] += dot_nn(query_t[:, r0 : r0 + count], grad_s)


def write_keys(refs, starts, dk_s, dv_s):
    for ref, c0 in zip(refs, starts):
        n = ref.shape[1]
        ref[0] = jnp.transpose(dk_s[:, c0 : c0 + n] * SCALE).astype(ref.dtype)
        ref[1] = jnp.transpose(dv_s[:, c0 : c0 + n]).astype(ref.dtype)


def far_kernel(
    info, q0, q1, q2, q3, g0, g1, g2, g3, gain_ref, sums, o_ref, l_ref, e_ref, p2, p3,
    n0, n1, n2, n3, dq_ref, d_p2, d_p3, q_s, g_s, dk_s, dv_s, r_s, c_s,
):
    x, z = info[0], info[1]
    head = pl.program_id(0)

    @pl.when(head == 0)
    def _():
        dk_s[...] = jnp.zeros_like(dk_s)
        dv_s[...] = jnp.zeros_like(dv_s)
        fill_columns(sums, r_s, c_s)

    for d, ref in enumerate((n0, n1, n2, n3)):
        rows = slot(x, d)
        ref[...] = (o_ref[head, rows, :] * r_s[rows, :] * gain_ref[...]).astype(bf16)

    @pl.when(z < 2)
    def _():
        dq_ref[head] = jnp.zeros((512, HD), f32)

    for reach in (2, 3):

        @pl.when(z == reach)
        def _():
            for d, (a, b) in enumerate(((q0, g0), (q1, g1), (q2, g2), (q3, g3))):
                q_s[slot(x, d), :] = a[...]
                g_s[slot(x, d), :] = b[...]
            rows_of = cotangent_rows(q_s, g_s, gain_ref, r_s, c_s, o_ref, l_ref)
            spans = [(p2, 0, 512, 0, 0, 512), (p3, 0, 512, PAST, 0, 512)][: reach - 1]
            grad_q = [None, None]
            spans_back(spans, e_ref, rows_of, grad_q, dk_s, dv_s)
            dq_ref[head] = jnp.concatenate(grad_q, axis=0)

    @pl.when((head == GROUP - 1) & (z > 1))
    def _():
        write_keys((d_p2, d_p3), (0, PAST), dk_s, dv_s)


def backward_far(info, parts, gain, sums, output, totals, weights, p2, p3):
    return pl.pallas_call(
        far_kernel,
        name="backward_far",
        grid_spec=pltpu.PrefetchScalarGridSpec(
            num_scalar_prefetch=1,
            grid=(GROUP,),
            in_specs=[per_head(128)] * 4
            + [per_head(128, 1)] * 4
            + [per_head(1), all_of(8, 128), KEPT, KEPT, KEPT]
            + [all_of(2, 512, 128)] * 2,
            out_specs=[per_head(128)] * 4 + [KEPT] + [all_of(2, 512, 128)] * 2,
            scratch_shapes=[pltpu.VMEM((512, 128), bf16)] * 2
            + [pltpu.VMEM((128, FAR), f32)] * 2
            + [pltpu.VMEM((512, 128), f32)] * 2,
        ),
        out_shape=[jax.ShapeDtypeStruct((128, GROUP * HD), bf16)] * 4
        + [pltpu.VMEM((GROUP, 512, HD), f32)]
        + [jax.ShapeDtypeStruct((2, 512, 128), bf16)] * 2,
        compiler_params=LIMIT,
    )(info, *parts, *parts, gain, sums, output, totals, weights, p2, p3)


def near_kernel(
    info, q0, q1, q2, q3, g0, g1, g2, g3, gain_ref, sums, o_ref, l_ref, e_ref, dq_ref,
    own, halo, p1,
    dq0, dq1, dq2, dq3, d_own, d_halo, d_p1, q_s, g_s, dq_s, dk_s, dv_s, r_s, c_s,
):
    x, z = info[0], info[1]
    head = pl.program_id(0)
    for d, (a, b) in enumerate(((q0, g0), (q1, g1), (q2, g2), (q3, g3))):
        q_s[slot(x, d), :] = a[...]
        g_s[slot(x, d), :] = b[...]

    @pl.when(head == 0)
    def _():
        dk_s[...] = jnp.zeros_like(dk_s)
        dv_s[...] = jnp.zeros_like(dv_s)
        fill_columns(sums, r_s, c_s)

    rows_of = cotangent_rows(q_s, g_s, gain_ref, r_s, c_s, o_ref, l_ref)

    def body(reach):
        spans = [
            (own, 0, 384, 0, 0, 256),
            (own, 0, 512, 0, 256, 256),
            (halo, 0, 128, OWN, 256, 256),
        ]
        if reach:
            spans.append((p1, 0, 512, OWN + HALO, 0, 512))
        grad_q = [dq_ref[head, 0:256, :], dq_ref[head, 256:512, :]]
        spans_back(spans, e_ref, rows_of, grad_q, dk_s, dv_s)
        dq_s[...] = (jnp.concatenate(grad_q, axis=0) * SCALE).astype(bf16)

    @pl.when(z == 0)
    def _():
        body(0)

    @pl.when(z > 0)
    def _():
        body(1)

    for d, ref in enumerate((dq0, dq1, dq2, dq3)):
        ref[...] = dq_s[slot(x, d), :]

    @pl.when(head == GROUP - 1)
    def _():
        write_keys((d_own, d_halo, d_p1), (0, OWN, OWN + HALO), dk_s, dv_s)


def backward_near(info, parts, gain, sums, output, totals, weights, dq, own, halo, p1):
    return pl.pallas_call(
        near_kernel,
        name="backward_near",
        grid_spec=pltpu.PrefetchScalarGridSpec(
            num_scalar_prefetch=1,
            grid=(GROUP,),
            in_specs=[per_head(128)] * 4
            + [per_head(128, 1)] * 4
            + [per_head(1), all_of(8, 128), KEPT, KEPT, KEPT]
            + [KEPT, all_of(2, 512, 128), all_of(272, 128), all_of(2, 512, 128)],
            out_specs=[per_head(128)] * 4
            + [all_of(2, 512, 128), all_of(2, 128, 128), all_of(2, 512, 128)],
            scratch_shapes=[pltpu.VMEM((512, 128), bf16)] * 3
            + [pltpu.VMEM((128, NEAR), f32)] * 2
            + [pltpu.VMEM((512, 128), f32)] * 2,
        ),
        out_shape=[jax.ShapeDtypeStruct((128, GROUP * HD), bf16)] * 4
        + [
            jax.ShapeDtypeStruct((2, 512, 128), f32),
            jax.ShapeDtypeStruct((2, 128, 128), bf16),
            jax.ShapeDtypeStruct((2, 512, 128), bf16),
        ],
        compiler_params=LIMIT,
    )(info, *parts, *parts, gain, sums, output, totals, weights, dq, own, halo, p1)


def along(x, axis, pairs):
    return lax.ppermute(x, axis, pairs)


def unit_of(block, unit):
    return lax.dynamic_slice(
        block, (unit // 2, 0, (unit % 2) * GROUP * HD), (1, 128, GROUP * HD)
    )[0]


def to_units(first, second, x):
    parts = []
    for d in range(4):
        unit = (x + d) & 3
        part = jnp.concatenate([unit_of(first, unit), unit_of(second, unit)], axis=0)
        parts.append(
            part if d == 0 else along(part, "ctx_1", [(i, (i + d) % 4) for i in range(4)])
        )
    return parts


def from_units(parts, x):
    got = [parts[0]]
    for d in range(1, 4):
        got.append(along(parts[d], "ctx_1", [(i, (i - d) % 4) for i in range(4)]))
    units = jnp.stack(got)
    units = jnp.stack([lax.dynamic_index_in_dim(units, (u - x) & 3, 0, False) for u in range(4)])
    units = units.reshape(2, 2, 128, GROUP * HD)
    return jnp.concatenate([units[:, 0], units[:, 1]], axis=-1)


def section_route(d, sign):
    route = []
    for s in range(4):
        for i in range(4):
            if sign > 0:
                unit = (i + d) % 4
                route.append((s * 4 + i, (s + unit // 2) % 4 * 4 + unit))
            else:
                route.append((s * 4 + i, (s - i // 2) % 4 * 4 + (i - d) % 4))
    return route


def whole_step(query_heads, keys_values, grad_output, norm_gain, turn_ids):
    z = lax.axis_index("ctx_0")
    x = lax.axis_index("ctx_1")
    info = jnp.stack([x, z]).astype(jnp.int32)

    turn_rows = jnp.broadcast_to(turn_ids.astype(bf16)[None], (16, 128))
    kv = keys_values[0]
    heads = [
        jnp.concatenate([kv[:, 0, a : a + HD], kv[:, 1, a : a + HD], turn_rows], axis=0)
        for a in (0, HD)
    ]
    odd = (x & 1) == 1
    same = jnp.where(odd, heads[1], heads[0])
    other = jnp.where(odd, heads[0], heads[1])
    received = [
        along(same if d % 2 == 0 else other, ("section", "ctx_1"), section_route(d, 1))
        for d in range(4)
    ]
    parts = to_units(query_heads[0], grad_output[0], x)
    own, first, turns = put_in_order(info, received)
    halo = along(first, "ctx_0", [(1, 0), (2, 1), (3, 2)])
    past2 = along(own, "ctx_0", [(0, 2), (1, 3)])
    past1 = along(own, "ctx_0", [(0, 1), (1, 2), (2, 3)])
    past3 = along(past2, "ctx_0", [(2, 3)])
    gain = lax.dynamic_slice(norm_gain[0], (x // 2, (x % 2) * GROUP * HD), (1, GROUP * HD))

    output, totals, near, far, sums = forward(
        info, parts, gain, turns, own, halo, (past1, past2, past3)
    )
    sums = sums + along(sums, "tp", [(i, i ^ 1) for i in range(4)])
    sums = sums + along(sums, "ctx_1", [(i, i ^ 1) for i in range(4)])
    sums = sums + along(sums, "tp", [(i, i ^ 2) for i in range(4)])

    results = backward_far(info, parts, gain, sums, output, totals, far, past2, past3)
    d_p2, d_p3 = results[5:]
    back3 = along(d_p3, "ctx_0", [(3, 0)])
    back2 = along(d_p2, "ctx_0", [(2, 0), (3, 1)])
    normed = from_units(results[:4], x)
    results = backward_near(
        info, parts, gain, sums, output, totals, near, results[4], own, halo, past1
    )
    d_own, d_halo, d_p1 = results[4:]
    back1 = along(d_p1, "ctx_0", [(1, 0), (2, 1), (3, 2)])
    front = along(d_halo, "ctx_0", [(0, 1), (1, 2), (2, 3)])
    grad_q = from_units(results[:4], x)
    total = d_own + back1.astype(f32) + back2.astype(f32) + back3.astype(f32)
    total = total + jnp.pad(front.astype(f32), ((0, 0), (0, 384), (0, 0)))
    total = total.astype(bf16).reshape(2, 4, 128, HD)
    returned = []
    for d in range(4):
        part = lax.dynamic_index_in_dim(total, (x - d) & 3, 1, False)
        returned.append(along(part, ("section", "ctx_1"), section_route(d, -1)))
    alike = returned[0].astype(f32) + returned[2].astype(f32)
    differ = returned[1].astype(f32) + returned[3].astype(f32)
    low = jnp.where(odd, differ, alike)
    high = jnp.where(odd, alike, differ)
    kv_grad = jnp.concatenate([low, high], axis=-1).transpose(1, 0, 2)
    return normed[None], grad_q[None], kv_grad[None]


def solution(mesh):
    split = Mesh(
        mesh.devices.reshape(mesh.shape["section"], 4, 4, mesh.shape["tp"]),
        ("section", "ctx_0", "ctx_1", "tp"),
    )
    return jax.shard_map(
        whole_step,
        mesh=split,
        in_specs=(
            P("section", None, CTX, "tp"),
            P("section", CTX, None, "tp"),
            P("section", None, CTX, "tp"),
            P("section", None, "tp"),
            P(CTX),
        ),
        out_specs=(
            P("section", None, CTX, "tp"),
            P("section", None, CTX, "tp"),
            P("section", CTX, None, "tp"),
        ),
        check_vma=False,
    )
```

time: 145 us -> 145 us (level)
  waiting for transfers between devices: 35.9 us -> 48.4 us
  Pallas kernels: 31.7 us -> 20.4 us
    ppermute x31 -> x28, waiting for transfers between devices: 35.9 us -> 48.4 us  [along(): return lax.ppermute(x, axis, pairs)]
    pallas_call x3 -> x2, Pallas kernels: 19.3 us -> 11.6 us  [the longest x1 9.46 us: backward_near(): pl.pallas_call(near_kernel, name='backward_near', grid_spec=pltpu.Prefetc...]
    pallas_call x1, Pallas kernels: 10.6 us -> 7.07 us  [forward(): pl.pallas_call(forward_kernel, name='attention_forward', grid_spec=pltpu....]
    concatenate x0 -> x4, other arithmetic: none -> 1.6 us  [to_units(): jnp.concatenate([unit_of(first, unit), unit_of(second, unit)], axis=0)]
    unnamed x47 -> x29, local copies, waits for them, and re-layouts: 3.24 us -> 2.97 us
    ppermute x31 -> x28, starting transfers between devices: 63.3 us -> 63.4 us  [along(): return lax.ppermute(x, axis, pairs)]
  transfers between devices with their start and end apart: 31 -> 28, of which waited for: 11 -> 12; matrix products, arithmetic and copies ran while one was open for 4% -> 4% of each run, Pallas kernels for 17% -> 1%
where the time goes in v2:
time: 145 us; the launch traced here: 144 us
  starting transfers between devices  63.4 us (44%)
  waiting for transfers between devices  48.4 us (33%)
  Pallas kernels  20.4 us (14%)
  other arithmetic  6.13 us (4%)
  local copies, waits for them, and re-layouts  4.96 us (3%)
    ppermute x28, starting transfers between devices, along(): return lax.ppermute(x, axis, pairs)  63.4 us
    ppermute x28, waiting for transfers between devices, along(): return lax.ppermute(x, axis, pairs)  48.4 us
    pallas_call x1, Pallas kernels, backward_near(): pl.pallas_call(near_kernel, name='backward_near', grid_spec=pltpu.Prefetc...  9.46 us
    pallas_call x1, Pallas kernels, forward(): pl.pallas_call(forward_kernel, name='attention_forward', grid_spec=pltpu....  7.07 us
    unnamed x29, local copies, waits for them, and re-layouts  2.97 us
  transfers between devices with their start and end apart: 28, of which 12 were waited for; matrix products, arithmetic and copies ran while one was open for 4% of the time, Pallas kernels for 1%

profile of v2, /device:TPU:4, one launch (start us, length us, event | category | flops | bytes accessed | tf_op | source)
XLA Modules:
  0.0 144.3 jit_solution(9440632605738095521)
XLA Ops:
  2.4 3.5 %collective-permute-start.3 = (bf16[272,128]{1,0:T(8,128)(2,1)S(1)}, bf16[272,128]{1,0:T(8,128)(2,1)S(1)}, u32[]{:S(2)}, u32[]{:S(2)}) collective-permute-start(bf16[272,128]{1,0:T(8,128)(2,1)S(1)} %get-tuple-element.74), channel_id=1, source_target_pairs={{0,0},{4,4},{8,72},{12,76},{64,64},{68,68},{72,136},{76,140},{128,... | collective-permute-start | bytes 208904 | tf_op jit(solution)/shard_map/ppermute | solution.py:398
  6.0 2.3 %collective-permute-start.4 = (bf16[272,128]{1,0:T(8,128)(2,1)S(1)}, bf16[272,128]{1,0:T(8,128)(2,1)S(1)}, u32[]{:S(2)}, u32[]{:S(2)}) collective-permute-start(bf16[272,128]{1,0:T(8,128)(2,1)S(1)} %get-tuple-element.73), channel_id=1, source_target_pairs={{0,4},{4,72},{8,76},{12,0},{64,68},{68,136},{72,140},{76,64},{128,... | collective-permute-start | bytes 208904 | tf_op jit(solution)/shard_map/ppermute | solution.py:398
  8.3 1.4 collective-permute-start.6
  9.6 1.3 dynamic-slice_bitcast_fusion
  11.8 2.0 %collective-permute-start.2 = (bf16[256,768]{1,0:T(8,128)(2,1)}, bf16[256,768]{1,0:T(8,128)(2,1)S(1)}, u32[]{:S(2)}, u32[]{:S(2)}) collective-permute-start(bf16[256,768]{1,0:T(8,128)(2,1)} %pad_maximum_fusion.7), channel_id=1, source_target_pairs={{0,12},{4,0},{8,4},{12,8},{1,13},{5,1},{9,5},{13,9},{2,14},{6,2},{... | collective-permute-start | bytes 1179656 | tf_op jit(solution)/shard_map/ppermute | solution.py:398
  16.1 1.8 %order_keys.1 = (bf16[2,512,128]{2,1,0:T(8,128)(2,1)}, bf16[272,128]{1,0:T(8,128)(2,1)}, f32[8,128]{1,0:T(8,128)}) custom-call(s32[2]{0:T(128)} %pad_add_fusion.info, bf16[272,128]{1,0:T(8,128)(2,1)} %copy-done.9, bf16[272,128]{1,0:T(8,128)(2,1)} %copy-done.11, bf16[272,128]{1,0:T(8,128)(2,1)} %copy-done.10, bf16[272,128]{1,0:T(8,128)(2,1)} %copy-done.12), custom_call_target="tpu_custom_call" | custom-call | tf_op jit(solution)/shard_map/order_keys/pallas_call | solution.py:61
  17.9 5.3 %collective-permute-start.9 = (bf16[2,512,128]{2,1,0:T(8,128)(2,1)}, bf16[2,512,128]{2,1,0:T(8,128)(2,1)S(1)}, u32[]{:S(2)}, u32[]{:S(2)}) collective-permute-start(bf16[2,512,128]{2,1,0:T(8,128)(2,1)} %get-tuple-element.26.own), channel_id=1, source_target_pairs={{0,32},{16,48},{1,33},{17,49},{2,34},{18,50},{3,35},{19,51},{4,36}... | collective-permute-start | bytes 786440 | tf_op jit(solution)/shard_map/ppermute | solution.py:398
  23.2 2.5 %collective-permute-start.1 = (bf16[256,768]{1,0:T(8,128)(2,1)S(1)}, bf16[256,768]{1,0:T(8,128)(2,1)S(1)}, u32[]{:S(2)}, u32[]{:S(2)}) collective-permute-start(bf16[256,768]{1,0:T(8,128)(2,1)S(1)} %pad_maximum_fusion.6), channel_id=1, source_target_pairs={{0,8},{4,12},{8,0},{12,4},{1,9},{5,13},{9,1},{13,5},{2,10},{6,14},... | collective-permute-start | bytes 1179656 | tf_op jit(solution)/shard_map/ppermute | solution.py:398
  26.5 2.6 %collective-permute-start = (bf16[256,768]{1,0:T(8,128)(2,1)}, bf16[256,768]{1,0:T(8,128)(2,1)S(1)}, u32[]{:S(2)}, u32[]{:S(2)}) collective-permute-start(bf16[256,768]{1,0:T(8,128)(2,1)} %pad_maximum_fusion.5), channel_id=1, source_target_pairs={{0,4},{4,8},{8,12},{12,0},{1,5},{5,9},{9,13},{13,1},{2,6},{6,10},{... | collective-permute-start | bytes 1179656 | tf_op jit(solution)/shard_map/ppermute | solution.py:398
  29.1 1.3 collective-permute-start.7
  30.4 4.9 %collective-permute-done.7.halo = bf16[272,128]{1,0:T(8,128)(2,1)S(1)} collective-permute-done((bf16[272,128]{1,0:T(8,128)(2,1)S(1)}, bf16[272,128]{1,0:T(8,128)(2,1)S(1)}, u32[]{:S(2)}, u32[]{:S(2)}) %collective-permute-start.7) | collective-permute-done | bytes 69664 | tf_op jit(solution)/shard_map/ppermute | solution.py:398
  35.3 3.8 %collective-permute-start.8 = (bf16[2,512,128]{2,1,0:T(8,128)(2,1)S(1)}, bf16[2,512,128]{2,1,0:T(8,128)(2,1)S(1)}, u32[]{:S(2)}, u32[]{:S(2)}) collective-permute-start(bf16[2,512,128]{2,1,0:T(8,128)(2,1)S(1)} %copy-done.1), channel_id=1, source_target_pairs={{0,16},{16,32},{32,48},{1,17},{17,33},{33,49},{2,18},{18,34},{34,5... | collective-permute-start | bytes 786440 | tf_op jit(solution)/shard_map/ppermute | solution.py:398
  40.0 3.0 %collective-permute-done.8.p1 = bf16[2,512,128]{2,1,0:T(8,128)(2,1)S(1)} collective-permute-done((bf16[2,512,128]{2,1,0:T(8,128)(2,1)S(1)}, bf16[2,512,128]{2,1,0:T(8,128)(2,1)S(1)}, u32[]{:S(2)}, u32[]{:S(2)}) %collective-permute-start.8) | collective-permute-done | bytes 262176 | tf_op jit(solution)/shard_map/ppermute | solution.py:398
  43.0 7.1 %attention_forward.1 = (f32[6,512,128]{2,1,0:T(8,128)S(1)}, f32[6,512,128]{2,1,0:T(8,128)S(1)}, bf16[6,512,1152]{2,1,0:T(8,128)(2,1)S(1)}, bf16[6,512,1024]{2,1,0:T(8,128)(2,1)S(1)}, f32[8,128]{1,0:T(8,128)S(1)}) custom-call(s32[2]{0:T(128)S(1)} %copy-done.2, bf16[256,768]{1,0:T(8,128)(2,1)S(1)} %pad_maximum_fusion.4.q0.g0, ...), custom_call_target="tpu_custom_call" | custom-call | tf_op jit(solution)/shard_map/attention_forward/pallas_call | solution.py:189
  52.2 3.0 %collective-permute-done.12 = f32[8,128]{1,0:T(8,128)S(1)} collective-permute-done((f32[8,128]{1,0:T(8,128)S(1)}, f32[8,128]{1,0:T(8,128)S(1)}, u32[]{:S(2)}, u32[]{:S(2)}) %collective-permute-start.12) | collective-permute-done | bytes 4128 | tf_op jit(solution)/shard_map/ppermute | solution.py:398
  55.2 4.8 %collective-permute-start.13 = (f32[8,128]{1,0:T(8,128)S(1)}, f32[8,128]{1,0:T(8,128)S(1)}, u32[]{:S(2)}, u32[]{:S(2)}) collective-permute-start(f32[8,128]{1,0:T(8,128)S(1)} %add.153), channel_id=1, source_target_pairs={{0,2},{1,3},{2,0},{3,1},{4,6},{5,7},{6,4},{7,5},{8,10},{9,11},{10,... | collective-permute-start | bytes 12296 | tf_op jit(solution)/shard_map/ppermute | solution.py:398
  60.0 2.7 %collective-permute-done.13 = f32[8,128]{1,0:T(8,128)S(1)} collective-permute-done((f32[8,128]{1,0:T(8,128)S(1)}, f32[8,128]{1,0:T(8,128)S(1)}, u32[]{:S(2)}, u32[]{:S(2)}) %collective-permute-start.13) | collective-permute-done | bytes 4128 | tf_op jit(solution)/shard_map/ppermute | solution.py:398
  62.7 2.1 %backward_far.1 = (bf16[128,768]{1,0:T(8,128)(2,1)S(1)}, bf16[128,768]{1,0:T(8,128)(2,1)S(1)}, bf16[128,768]{1,0:T(8,128)(2,1)S(1)}, bf16[128,768]{1,0:T(8,128)(...) custom-call(s32[2]{0:T(128)S(1)} %copy-done.2, ...), custom_call_target="tpu_custom_call" | custom-call | tf_op jit(solution)/shard_map/backward_far/pallas_call | solution.py:301
  65.5 9.5 %backward_near.1 = (bf16[128,768]{1,0:T(8,128)(2,1)S(1)}, bf16[128,768]{1,0:T(8,128)(2,1)}, bf16[128,768]{1,0:T(8,128)(2,1)}, bf16[128,768]{1,0:T(8,128)(2,1)}, ...) custom-call(s32[2]{0:T(128)S(1)} %copy-done.2, ...), custom_call_target="tpu_custom_call" | custom-call | tf_op jit(solution)/shard_map/backward_near/pallas_call | solution.py:371
  76.3 2.0 %collective-permute-start.18 = (bf16[128,768]{1,0:T(8,128)(2,1)}, bf16[128,768]{1,0:T(8,128)(2,1)S(1)}, u32[]{:S(2)}, u32[]{:S(2)}) collective-permute-start(bf16[128,768]{1,0:T(8,128)(2,1)} %get-tuple-element.40), channel_id=1, source_target_pairs={{0,8},{4,12},{8,0},{12,4},{1,9},{5,13},{9,1},{13,5},{2,10},{6,14},... | collective-permute-start | bytes 589832 | tf_op jit(solution)/shard_map/ppermute | solution.py:398
  78.3 2.1 %collective-permute-start.19 = (bf16[128,768]{1,0:T(8,128)(2,1)}, bf16[128,768]{1,0:T(8,128)(2,1)S(1)}, u32[]{:S(2)}, u32[]{:S(2)}) collective-permute-start(bf16[128,768]{1,0:T(8,128)(2,1)} %get-tuple-element.41), channel_id=1, source_target_pairs={{0,4},{4,8},{8,12},{12,0},{1,5},{5,9},{9,13},{13,1},{2,6},{6,10},{... | collective-permute-start | bytes 589832 | tf_op jit(solution)/shard_map/ppermute | solution.py:398
  80.4 1.3 collective-permute-start.20
  81.6 10.0 %collective-permute-start.23 = (bf16[2,128,128]{2,1,0:T(8,128)(2,1)}, bf16[2,128,128]{2,1,0:T(8,128)(2,1)S(1)}, u32[]{:S(2)}, u32[]{:S(2)}) collective-permute-start(bf16[2,128,128]{2,1,0:T(8,128)(2,1)} %copy-done.7), channel_id=1, source_target_pairs={{0,16},{16,32},{32,48},{1,17},{17,33},{33,49},{2,18},{18,34},{34,5... | collective-permute-start | bytes 196616 | tf_op jit(solution)/shard_map/ppermute | solution.py:398
  91.8 2.7 %collective-permute-start.15 = (bf16[128,768]{1,0:T(8,128)(2,1)}, bf16[128,768]{1,0:T(8,128)(2,1)S(1)}, u32[]{:S(2)}, u32[]{:S(2)}) collective-permute-start(bf16[128,768]{1,0:T(8,128)(2,1)} %copy-done.5), channel_id=1, source_target_pairs={{0,8},{4,12},{8,0},{12,4},{1,9},{5,13},{9,1},{13,5},{2,10},{6,14},... | collective-permute-start | bytes 589832 | tf_op jit(solution)/shard_map/ppermute | solution.py:398
  94.9 2.7 %collective-permute-done.14 = bf16[128,768]{1,0:T(8,128)(2,1)S(1)} collective-permute-done((bf16[128,768]{1,0:T(8,128)(2,1)}, bf16[128,768]{1,0:T(8,128)(2,1)S(1)}, u32[]{:S(2)}, u32[]{:S(2)}) %collective-permute-start.14) | collective-permute-done | bytes 196640 | tf_op jit(solution)/shard_map/ppermute | solution.py:398
  97.7 1.3 collective-permute-start.21
  99.4 1.3 collective-permute-start.22
  102.7 26.2 %collective-permute-done.21 = bf16[2,512,128]{2,1,0:T(8,128)(2,1)S(1)} collective-permute-done((bf16[2,512,128]{2,1,0:T(8,128)(2,1)S(1)}, bf16[2,512,128]{2,1,0:T(8,128)(2,1)S(1)}, u32[]{:S(2)}, u32[]{:S(2)}) %collective-permute-start.21) | collective-permute-done | bytes 262176 | tf_op jit(solution)/shard_map/ppermute | solution.py:398
  129.1 5.8 %collective-permute-start.25 = (bf16[2,128,128]{2,0,1:T(2,128)(2,1)S(1)}, bf16[2,128,128]{2,0,1:T(2,128)(2,1)S(1)}, u32[]{:S(2)}, u32[]{:S(2)}) collective-permute-start(bf16[2,128,128]{2,0,1:T(2,128)(2,1)S(1)} %bitcast.102), channel_id=1, source_target_pairs={{0,4},{4,8},{8,204},{12,192},{64,68},{68,72},{72,12},{76,0},{128,1... | collective-permute-start | bytes 196616 | tf_op jit(solution)/shard_map/ppermute | solution.py:398
  135.1 2.1 %collective-permute-start.27 = (bf16[2,128,128]{2,0,1:T(2,128)(2,1)S(1)}, bf16[2,128,128]{2,0,1:T(2,128)(2,1)S(1)}, u32[]{:S(2)}, u32[]{:S(2)}) collective-permute-start(bf16[2,128,128]{2,0,1:T(2,128)(2,1)S(1)} %bitcast.104), channel_id=1, source_target_pairs={{0,8},{4,12},{8,192},{12,196},{64,72},{68,76},{72,0},{76,4},{128,1... | collective-permute-start | bytes 196616 | tf_op jit(solution)/shard_map/ppermute | solution.py:398
  137.3 2.7 %collective-permute-start.26 = (bf16[2,128,128]{2,0,1:T(2,128)(2,1)S(1)}, bf16[2,128,128]{2,0,1:T(2,128)(2,1)S(1)}, u32[]{:S(2)}, u32[]{:S(2)}) collective-permute-start(bf16[2,128,128]{2,0,1:T(2,128)(2,1)S(1)} %bitcast.105), channel_id=1, source_target_pairs={{0,0},{4,4},{8,200},{12,204},{64,64},{68,68},{72,8},{76,12},{128,1... | collective-permute-start | bytes 196616 | tf_op jit(solution)/shard_map/ppermute | solution.py:398
  141.0 2.5 %collective-permute-done.26 = bf16[2,128,128]{2,0,1:T(2,128)(2,1)S(1)} collective-permute-done((bf16[2,128,128]{2,0,1:T(2,128)(2,1)S(1)}, bf16[2,128,128]{2,0,1:T(2,128)(2,1)S(1)}, u32[]{:S(2)}, u32[]{:S(2)}) %collective-permute-start.26) | collective-permute-done | bytes 65568 | tf_op jit(solution)/shard_map/ppermute | solution.py:398
  (89 shorter events, 15.8 us)
Async XLA Ops:
  0.6 39.2 %copy-start = (f32[1,2,1536]{2,1,0:T(2,128)S(1)}, f32[1,2,1536]{2,1,0:T(2,128)}, u32[]{:S(2)}) copy-start(f32[1,2,1536]{2,1,0:T(2,128)} %param.8) | copy-start | bytes 36868
  2.4 12.0 %collective-permute-start.3 = (bf16[272,128]{1,0:T(8,128)(2,1)S(1)}, bf16[272,128]{1,0:T(8,128)(2,1)S(1)}, u32[]{:S(2)}, u32[]{:S(2)}) collective-permute-start(bf16[272,128]{1,0:T(8,128)(2,1)S(1)} %get-tuple-element.74), channel_id=1, source_target_pairs={{0,0},{4,4},{8,72},{12,76},{64,64},{68,68},{72,136},{76,140},{128,... | collective-permute-start | bytes 208904 | tf_op jit(solution)/shard_map/ppermute | solution.py:398
  5.9 8.8 %collective-permute-start.5 = (bf16[272,128]{1,0:T(8,128)(2,1)S(1)}, bf16[272,128]{1,0:T(8,128)(2,1)S(1)}, u32[]{:S(2)}, u32[]{:S(2)}) collective-permute-start(bf16[272,128]{1,0:T(8,128)(2,1)S(1)} %get-tuple-element.74), channel_id=1, source_target_pairs={{0,72},{4,76},{8,0},{12,4},{64,136},{68,140},{72,64},{76,68},{128,... | collective-permute-start | bytes 208904 | tf_op jit(solution)/shard_map/ppermute | solution.py:398
  6.0 8.4 %collective-permute-start.4 = (bf16[272,128]{1,0:T(8,128)(2,1)S(1)}, bf16[272,128]{1,0:T(8,128)(2,1)S(1)}, u32[]{:S(2)}, u32[]{:S(2)}) collective-permute-start(bf16[272,128]{1,0:T(8,128)(2,1)S(1)} %get-tuple-element.73), channel_id=1, source_target_pairs={{0,4},{4,72},{8,76},{12,0},{64,68},{68,136},{72,140},{76,64},{128,... | collective-permute-start | bytes 208904 | tf_op jit(solution)/shard_map/ppermute | solution.py:398
  8.3 7.2 %collective-permute-start.6 = (bf16[272,128]{1,0:T(8,128)(2,1)S(1)}, bf16[272,128]{1,0:T(8,128)(2,1)S(1)}, u32[]{:S(2)}, u32[]{:S(2)}) collective-permute-start(bf16[272,128]{1,0:T(8,128)(2,1)S(1)} %get-tuple-element.73), channel_id=1, source_target_pairs={{0,76},{4,0},{8,4},{12,72},{64,140},{68,64},{72,68},{76,136},{128,... | collective-permute-start | bytes 208904 | tf_op jit(solution)/shard_map/ppermute | solution.py:398
  11.8 31.2 %collective-permute-start.2 = (bf16[256,768]{1,0:T(8,128)(2,1)}, bf16[256,768]{1,0:T(8,128)(2,1)S(1)}, u32[]{:S(2)}, u32[]{:S(2)}) collective-permute-start(bf16[256,768]{1,0:T(8,128)(2,1)} %pad_maximum_fusion.7), channel_id=1, source_target_pairs={{0,12},{4,0},{8,4},{12,8},{1,13},{5,1},{9,5},{13,9},{2,14},{6,2},{... | collective-permute-start | bytes 1179656 | tf_op jit(solution)/shard_map/ppermute | solution.py:398
  14.4 28.6 %copy-start.2 = (s32[2]{0:T(128)S(1)}, s32[2]{0:T(128)}, u32[]{:S(2)}) copy-start(s32[2]{0:T(128)} %pad_add_fusion.info) | copy-start | bytes 28
  17.9 17.4 %copy-start.1 = (bf16[2,512,128]{2,1,0:T(8,128)(2,1)S(1)}, bf16[2,512,128]{2,1,0:T(8,128)(2,1)}, u32[]{:S(2)}) copy-start(bf16[2,512,128]{2,1,0:T(8,128)(2,1)} %get-tuple-element.26.own) | copy-start | bytes 786436
  17.9 25.2 %copy-start.3 = (f32[8,128]{1,0:T(8,128)S(1)}, f32[8,128]{1,0:T(8,128)}, u32[]{:S(2)}) copy-start(f32[8,128]{1,0:T(8,128)} %get-tuple-element.25.turns) | copy-start | bytes 12292
  17.9 21.3 %collective-permute-start.9 = (bf16[2,512,128]{2,1,0:T(8,128)(2,1)}, bf16[2,512,128]{2,1,0:T(8,128)(2,1)S(1)}, u32[]{:S(2)}, u32[]{:S(2)}) collective-permute-start(bf16[2,512,128]{2,1,0:T(8,128)(2,1)} %get-tuple-element.26.own), channel_id=1, source_target_pairs={{0,32},{16,48},{1,33},{17,49},{2,34},{18,50},{3,35},{19,51},{4,36}... | collective-permute-start | bytes 786440 | tf_op jit(solution)/shard_map/ppermute | solution.py:398
  23.2 19.8 %collective-permute-start.1 = (bf16[256,768]{1,0:T(8,128)(2,1)S(1)}, bf16[256,768]{1,0:T(8,128)(2,1)S(1)}, u32[]{:S(2)}, u32[]{:S(2)}) collective-permute-start(bf16[256,768]{1,0:T(8,128)(2,1)S(1)} %pad_maximum_fusion.6), channel_id=1, source_target_pairs={{0,8},{4,12},{8,0},{12,4},{1,9},{5,13},{9,1},{13,5},{2,10},{6,14},... | collective-permute-start | bytes 1179656 | tf_op jit(solution)/shard_map/ppermute | solution.py:398
  26.5 16.5 %collective-permute-start = (bf16[256,768]{1,0:T(8,128)(2,1)}, bf16[256,768]{1,0:T(8,128)(2,1)S(1)}, u32[]{:S(2)}, u32[]{:S(2)}) collective-permute-start(bf16[256,768]{1,0:T(8,128)(2,1)} %pad_maximum_fusion.5), channel_id=1, source_target_pairs={{0,4},{4,8},{8,12},{12,0},{1,5},{5,9},{9,13},{13,1},{2,6},{6,10},{... | collective-permute-start | bytes 1179656 | tf_op jit(solution)/shard_map/ppermute | solution.py:398
  29.1 6.2 %collective-permute-start.7 = (bf16[272,128]{1,0:T(8,128)(2,1)S(1)}, bf16[272,128]{1,0:T(8,128)(2,1)S(1)}, u32[]{:S(2)}, u32[]{:S(2)}) collective-permute-start(bf16[272,128]{1,0:T(8,128)(2,1)S(1)} %copy-done.13), channel_id=1, source_target_pairs={{16,0},{32,16},{48,32},{17,1},{33,17},{49,33},{18,2},{34,18},{50,3... | collective-permute-start | bytes 208904 | tf_op jit(solution)/shard_map/ppermute | solution.py:398
  35.3 7.7 %collective-permute-start.8 = (bf16[2,512,128]{2,1,0:T(8,128)(2,1)S(1)}, bf16[2,512,128]{2,1,0:T(8,128)(2,1)S(1)}, u32[]{:S(2)}, u32[]{:S(2)}) collective-permute-start(bf16[2,512,128]{2,1,0:T(8,128)(2,1)S(1)} %copy-done.1), channel_id=1, source_target_pairs={{0,16},{16,32},{32,48},{1,17},{17,33},{33,49},{2,18},{18,34},{34,5... | collective-permute-start | bytes 786440 | tf_op jit(solution)/shard_map/ppermute | solution.py:398
  39.1 3.9 %collective-permute-start.10 = (bf16[2,512,128]{2,1,0:T(8,128)(2,1)S(1)}, bf16[2,512,128]{2,1,0:T(8,128)(2,1)S(1)}, u32[]{:S(2)}, u32[]{:S(2)}) collective-permute-start(bf16[2,512,128]{2,1,0:T(8,128)(2,1)S(1)} %collective-permute-done.9.p2), channel_id=1, source_target_pairs={{32,48},{33,49},{34,50},{35,51},{36,52},{37,53},{38,54},{39,55},{4... | collective-permute-start | bytes 786440 | tf_op jit(solution)/shard_map/ppermute | solution.py:398
  50.1 1.4 collective-permute-start.11
  51.5 3.6 %collective-permute-start.12 = (f32[8,128]{1,0:T(8,128)S(1)}, f32[8,128]{1,0:T(8,128)S(1)}, u32[]{:S(2)}, u32[]{:S(2)}) collective-permute-start(f32[8,128]{1,0:T(8,128)S(1)} %add.152), channel_id=1, source_target_pairs={{0,4},{4,0},{8,12},{12,8},{1,5},{5,1},{9,13},{13,9},{2,6},{6,2},{1... | collective-permute-start | bytes 12296 | tf_op jit(solution)/shard_map/ppermute | solution.py:398
  55.2 7.5 %collective-permute-start.13 = (f32[8,128]{1,0:T(8,128)S(1)}, f32[8,128]{1,0:T(8,128)S(1)}, u32[]{:S(2)}, u32[]{:S(2)}) collective-permute-start(f32[8,128]{1,0:T(8,128)S(1)} %add.153), channel_id=1, source_target_pairs={{0,2},{1,3},{2,0},{3,1},{4,6},{5,7},{6,4},{7,5},{8,10},{9,11},{10,... | collective-permute-start | bytes 12296 | tf_op jit(solution)/shard_map/ppermute | solution.py:398
  75.6 16.1 %collective-permute-start.17 = (bf16[128,768]{1,0:T(8,128)(2,1)}, bf16[128,768]{1,0:T(8,128)(2,1)S(1)}, u32[]{:S(2)}, u32[]{:S(2)}) collective-permute-start(bf16[128,768]{1,0:T(8,128)(2,1)} %get-tuple-element.39), channel_id=1, source_target_pairs={{0,12},{4,0},{8,4},{12,8},{1,13},{5,1},{9,5},{13,9},{2,14},{6,2},{... | collective-permute-start | bytes 589832 | tf_op jit(solution)/shard_map/ppermute | solution.py:398
  76.3 15.5 %collective-permute-start.18 = (bf16[128,768]{1,0:T(8,128)(2,1)}, bf16[128,768]{1,0:T(8,128)(2,1)S(1)}, u32[]{:S(2)}, u32[]{:S(2)}) collective-permute-start(bf16[128,768]{1,0:T(8,128)(2,1)} %get-tuple-element.40), channel_id=1, source_target_pairs={{0,8},{4,12},{8,0},{12,4},{1,9},{5,13},{9,1},{13,5},{2,10},{6,14},... | collective-permute-start | bytes 589832 | tf_op jit(solution)/shard_map/ppermute | solution.py:398
  78.3 16.2 %collective-permute-start.19 = (bf16[128,768]{1,0:T(8,128)(2,1)}, bf16[128,768]{1,0:T(8,128)(2,1)S(1)}, u32[]{:S(2)}, u32[]{:S(2)}) collective-permute-start(bf16[128,768]{1,0:T(8,128)(2,1)} %get-tuple-element.41), channel_id=1, source_target_pairs={{0,4},{4,8},{8,12},{12,0},{1,5},{5,9},{9,13},{13,1},{2,6},{6,10},{... | collective-permute-start | bytes 589832 | tf_op jit(solution)/shard_map/ppermute | solution.py:398
  80.4 22.3 %collective-permute-start.20 = (bf16[2,512,128]{2,1,0:T(8,128)(2,1)S(1)}, bf16[2,512,128]{2,1,0:T(8,128)(2,1)S(1)}, u32[]{:S(2)}, u32[]{:S(2)}) collective-permute-start(bf16[2,512,128]{2,1,0:T(8,128)(2,1)S(1)} %get-tuple-element.43), channel_id=1, source_target_pairs={{16,0},{32,16},{48,32},{17,1},{33,17},{49,33},{18,2},{34,18},{50,3... | collective-permute-start | bytes 786440 | tf_op jit(solution)/shard_map/ppermute | solution.py:398
  81.6 21.0 %collective-permute-start.23 = (bf16[2,128,128]{2,1,0:T(8,128)(2,1)}, bf16[2,128,128]{2,1,0:T(8,128)(2,1)S(1)}, u32[]{:S(2)}, u32[]{:S(2)}) collective-permute-start(bf16[2,128,128]{2,1,0:T(8,128)(2,1)} %copy-done.7), channel_id=1, source_target_pairs={{0,16},{16,32},{32,48},{1,17},{17,33},{33,49},{2,18},{18,34},{34,5... | collective-permute-start | bytes 196616 | tf_op jit(solution)/shard_map/ppermute | solution.py:398
  91.7 6.0 %collective-permute-start.14 = (bf16[128,768]{1,0:T(8,128)(2,1)}, bf16[128,768]{1,0:T(8,128)(2,1)S(1)}, u32[]{:S(2)}, u32[]{:S(2)}) collective-permute-start(bf16[128,768]{1,0:T(8,128)(2,1)} %copy-done.6), channel_id=1, source_target_pairs={{0,12},{4,0},{8,4},{12,8},{1,13},{5,1},{9,5},{13,9},{2,14},{6,2},{... | collective-permute-start | bytes 589832 | tf_op jit(solution)/shard_map/ppermute | solution.py:398
  91.8 7.6 %collective-permute-start.15 = (bf16[128,768]{1,0:T(8,128)(2,1)}, bf16[128,768]{1,0:T(8,128)(2,1)S(1)}, u32[]{:S(2)}, u32[]{:S(2)}) collective-permute-start(bf16[128,768]{1,0:T(8,128)(2,1)} %copy-done.5), channel_id=1, source_target_pairs={{0,8},{4,12},{8,0},{12,4},{1,9},{5,13},{9,1},{13,5},{2,10},{6,14},... | collective-permute-start | bytes 589832 | tf_op jit(solution)/shard_map/ppermute | solution.py:398
  94.5 6.9 %collective-permute-start.16 = (bf16[128,768]{1,0:T(8,128)(2,1)}, bf16[128,768]{1,0:T(8,128)(2,1)S(1)}, u32[]{:S(2)}, u32[]{:S(2)}) collective-permute-start(bf16[128,768]{1,0:T(8,128)(2,1)} %copy-done.4), channel_id=1, source_target_pairs={{0,4},{4,8},{8,12},{12,0},{1,5},{5,9},{9,13},{13,1},{2,6},{6,10},{... | collective-permute-start | bytes 589832 | tf_op jit(solution)/shard_map/ppermute | solution.py:398
  97.7 31.2 %collective-permute-start.21 = (bf16[2,512,128]{2,1,0:T(8,128)(2,1)S(1)}, bf16[2,512,128]{2,1,0:T(8,128)(2,1)S(1)}, u32[]{:S(2)}, u32[]{:S(2)}) collective-permute-start(bf16[2,512,128]{2,1,0:T(8,128)(2,1)S(1)} %get-tuple-element.44), channel_id=1, source_target_pairs={{32,0},{48,16},{33,1},{49,17},{34,2},{50,18},{35,3},{51,19},{36,4}... | collective-permute-start | bytes 786440 | tf_op jit(solution)/shard_map/ppermute | solution.py:398
  99.4 29.5 %collective-permute-start.22 = (bf16[2,512,128]{2,1,0:T(8,128)(2,1)S(1)}, bf16[2,512,128]{2,1,0:T(8,128)(2,1)S(1)}, u32[]{:S(2)}, u32[]{:S(2)}) collective-permute-start(bf16[2,512,128]{2,1,0:T(8,128)(2,1)S(1)} %get-tuple-element.45), channel_id=1, source_target_pairs={{48,0},{49,1},{50,2},{51,3},{52,4},{53,5},{54,6},{55,7},{56,8},{57... | collective-permute-start | bytes 786440 | tf_op jit(solution)/shard_map/ppermute | solution.py:398
  129.1 11.9 %collective-permute-start.25 = (bf16[2,128,128]{2,0,1:T(2,128)(2,1)S(1)}, bf16[2,128,128]{2,0,1:T(2,128)(2,1)S(1)}, u32[]{:S(2)}, u32[]{:S(2)}) collective-permute-start(bf16[2,128,128]{2,0,1:T(2,128)(2,1)S(1)} %bitcast.102), channel_id=1, source_target_pairs={{0,4},{4,8},{8,204},{12,192},{64,68},{68,72},{72,12},{76,0},{128,1... | collective-permute-start | bytes 196616 | tf_op jit(solution)/shard_map/ppermute | solution.py:398
  134.9 6.1 %collective-permute-start.24 = (bf16[2,128,128]{2,0,1:T(2,128)(2,1)S(1)}, bf16[2,128,128]{2,0,1:T(2,128)(2,1)S(1)}, u32[]{:S(2)}, u32[]{:S(2)}) collective-permute-start(bf16[2,128,128]{2,0,1:T(2,128)(2,1)S(1)} %bitcast.103), channel_id=1, source_target_pairs={{0,12},{4,0},{8,196},{12,200},{64,76},{68,64},{72,4},{76,8},{128,1... | collective-permute-start | bytes 196616 | tf_op jit(solution)/shard_map/ppermute | solution.py:398
  135.1 5.9 %collective-permute-start.27 = (bf16[2,128,128]{2,0,1:T(2,128)(2,1)S(1)}, bf16[2,128,128]{2,0,1:T(2,128)(2,1)S(1)}, u32[]{:S(2)}, u32[]{:S(2)}) collective-permute-start(bf16[2,128,128]{2,0,1:T(2,128)(2,1)S(1)} %bitcast.104), channel_id=1, source_target_pairs={{0,8},{4,12},{8,192},{12,196},{64,72},{68,76},{72,0},{76,4},{128,1... | collective-permute-start | bytes 196616 | tf_op jit(solution)/shard_map/ppermute | solution.py:398
  137.3 6.2 %collective-permute-start.26 = (bf16[2,128,128]{2,0,1:T(2,128)(2,1)S(1)}, bf16[2,128,128]{2,0,1:T(2,128)(2,1)S(1)}, u32[]{:S(2)}, u32[]{:S(2)}) collective-permute-start(bf16[2,128,128]{2,0,1:T(2,128)(2,1)S(1)} %bitcast.105), channel_id=1, source_target_pairs={{0,0},{4,4},{8,200},{12,204},{64,64},{68,68},{72,8},{76,12},{128,1... | collective-permute-start | bytes 196616 | tf_op jit(solution)/shard_map/ppermute | solution.py:398
  (10 other events, 44.0 us)

commit v3 on v2

--- a/solution.py
+++ b/solution.py
@@ -26,6 +26,11 @@
 f32 = jnp.float32
 
 
+KEPT = pl.BlockSpec(memory_space=pltpu.VMEM)
+SCALARS = pl.BlockSpec(memory_space=pltpu.SMEM)
+LIMIT = pltpu.CompilerParams(vmem_limit_bytes=28 << 20)
+
+
 def dot_nt(a, b):
     return lax.dot_general(a, b, (((1,), (1,)), ((), ())), preferred_element_type=f32)
 
@@ -64,15 +69,12 @@
         in_specs=[pl.BlockSpec(memory_space=pltpu.SMEM)] + [whole] * 4,
         out_specs=[whole] * 3,
         out_shape=[
-            jax.ShapeDtypeStruct((2, 512, 128), bf16),
-            jax.ShapeDtypeStruct((272, 128), bf16),
-            jax.ShapeDtypeStruct((8, 128), f32),
+            pltpu.VMEM((2, 512, 128), bf16),
+            pltpu.VMEM((272, 128), bf16),
+            pltpu.VMEM((8, 128), f32),
         ],
+        compiler_params=LIMIT,
     )(info, *parts)
-
-
-KEPT = pl.BlockSpec(memory_space=pltpu.VMEM)
-LIMIT = pltpu.CompilerParams(vmem_limit_bytes=28 << 20)
 
 
 def per_head(rows, at=0):
@@ -253,9 +255,9 @@
 
 def write_keys(refs, starts, dk_s, dv_s):
     for ref, c0 in zip(refs, starts):
-        n = ref.shape[1]
-        ref[0] = jnp.transpose(dk_s[:, c0 : c0 + n] * SCALE).astype(ref.dtype)
-        ref[1] = jnp.transpose(dv_s[:, c0 : c0 + n]).astype(ref.dtype)
+        n = ref.shape[2]
+        ref[0] = (dk_s[:, c0 : c0 + n] * SCALE).astype(ref.dtype)
+        ref[1] = dv_s[:, c0 : c0 + n].astype(ref.dtype)
 
 
 def far_kernel(
@@ -308,14 +310,14 @@
             + [per_head(128, 1)] * 4
             + [per_head(1), all_of(8, 128), KEPT, KEPT, KEPT]
             + [all_of(2, 512, 128)] * 2,
-            out_specs=[per_head(128)] * 4 + [KEPT] + [all_of(2, 512, 128)] * 2,
+            out_specs=[per_head(128)] * 4 + [KEPT] + [KEPT] * 2,
             scratch_shapes=[pltpu.VMEM((512, 128), bf16)] * 2
             + [pltpu.VMEM((128, FAR), f32)] * 2
             + [pltpu.VMEM((512, 128), f32)] * 2,
         ),
         out_shape=[jax.ShapeDtypeStruct((128, GROUP * HD), bf16)] * 4
         + [pltpu.VMEM((GROUP, 512, HD), f32)]
-        + [jax.ShapeDtypeStruct((2, 512, 128), bf16)] * 2,
+        + [pltpu.VMEM((2, 128, 512), bf16)] * 2,
         compiler_params=LIMIT,
     )(info, *parts, *parts, gain, sums, output, totals, weights, p2, p3)
 
@@ -379,19 +381,83 @@
             + [per_head(1), all_of(8, 128), KEPT, KEPT, KEPT]
             + [KEPT, all_of(2, 512, 128), all_of(272, 128), all_of(2, 512, 128)],
             out_specs=[per_head(128)] * 4
-            + [all_of(2, 512, 128), all_of(2, 128, 128), all_of(2, 512, 128)],
+            + [KEPT] * 3,
             scratch_shapes=[pltpu.VMEM((512, 128), bf16)] * 3
             + [pltpu.VMEM((128, NEAR), f32)] * 2
             + [pltpu.VMEM((512, 128), f32)] * 2,
         ),
         out_shape=[jax.ShapeDtypeStruct((128, GROUP * HD), bf16)] * 4
         + [
-            jax.ShapeDtypeStruct((2, 512, 128), f32),
-            jax.ShapeDtypeStruct((2, 128, 128), bf16),
-            jax.ShapeDtypeStruct((2, 512, 128), bf16),
+            pltpu.VMEM((2, 128, 512), f32),
+            pltpu.VMEM((2, 128, 128), bf16),
+            pltpu.VMEM((2, 128, 512), bf16),
         ],
         compiler_params=LIMIT,
     )(info, *parts, *parts, gain, sums, output, totals, weights, dq, own, halo, p1)
+
+
+def combine_kernel(info, own, back1, back2, back3, front, r0, r1, r2, r3, total):
+    x = info[0]
+    for c in range(4):
+        at = pl.ds(128 * c, 128)
+        part = own[:, :, at] + back1[:, :, at].astype(f32)
+        part = part + back2[:, :, at].astype(f32) + back3[:, :, at].astype(f32)
+        if c == 0:
+            part = part + front[...].astype(f32)
+        total[c] = part.astype(bf16)
+    for d, ref in enumerate((r0, r1, r2, r3)):
+        ref[...] = total[(x - d) & 3]
+
+
+def combine(info, own, back1, back2, back3, front):
+    return pl.pallas_call(
+        combine_kernel,
+        name="combine",
+        in_specs=[SCALARS] + [KEPT] * 5,
+        out_specs=[KEPT] * 4,
+        out_shape=[pltpu.VMEM((2, 128, 128), bf16)] * 4,
+        scratch_shapes=[pltpu.VMEM((4, 2, 128, 128), bf16)],
+        compiler_params=LIMIT,
+    )(info, own, back1, back2, back3, front)
+
+
+def finish_kernel(info, r0, r1, r2, r3, out):
+    x = info[0]
+    for a, b, flip in ((r0, r2, 0), (r1, r3, 1)):
+        at = pl.ds(pl.multiple_of(((x + flip) & 1) * 128, 128), 128)
+        for half in range(2):
+            both = a[half].astype(f32) + b[half].astype(f32)
+            out[half, :, at] = jnp.transpose(both)
+
+
+def finish(info, parts):
+    return pl.pallas_call(
+        finish_kernel,
+        name="finish",
+        in_specs=[SCALARS] + [KEPT] * 4,
+        out_specs=KEPT,
+        out_shape=pltpu.VMEM((2, 128, 256), f32),
+        compiler_params=LIMIT,
+    )(info, *parts)
+
+
+def gather_kernel(info, r0, r1, r2, r3, out):
+    x = info[0]
+    for d, ref in enumerate((r0, r1, r2, r3)):
+        unit = (x + d) & 3
+        at = pl.ds(pl.multiple_of((unit & 1) * GROUP * HD, 128), GROUP * HD)
+        out[unit >> 1, :, at] = ref[...]
+
+
+def gather(info, parts):
+    return pl.pallas_call(
+        gather_kernel,
+        name="gather",
+        in_specs=[SCALARS] + [KEPT] * 4,
+        out_specs=KEPT,
+        out_shape=jax.ShapeDtypeStruct((2, 128, 2 * GROUP * HD), bf16),
+        compiler_params=LIMIT,
+    )(info, *parts)
 
 
 def along(x, axis, pairs):
@@ -415,14 +481,11 @@
     return parts
 
 
-def from_units(parts, x):
+def from_units(parts, info):
     got = [parts[0]]
     for d in range(1, 4):
         got.append(along(parts[d], "ctx_1", [(i, (i - d) % 4) for i in range(4)]))
-    units = jnp.stack(got)
-    units = jnp.stack([lax.dynamic_index_in_dim(units, (u - x) & 3, 0, False) for u in range(4)])
-    units = units.reshape(2, 2, 128, GROUP * HD)
-    return jnp.concatenate([units[:, 0], units[:, 1]], axis=-1)
+    return gather(info, got)
 
 
 def section_route(d, sign):
@@ -474,26 +537,20 @@
     d_p2, d_p3 = results[5:]
     back3 = along(d_p3, "ctx_0", [(3, 0)])
     back2 = along(d_p2, "ctx_0", [(2, 0), (3, 1)])
-    normed = from_units(results[:4], x)
+    normed = from_units(results[:4], info)
     results = backward_near(
         info, parts, gain, sums, output, totals, near, results[4], own, halo, past1
     )
     d_own, d_halo, d_p1 = results[4:]
     back1 = along(d_p1, "ctx_0", [(1, 0), (2, 1), (3, 2)])
     front = along(d_halo, "ctx_0", [(0, 1), (1, 2), (2, 3)])
-    grad_q = from_units(results[:4], x)
-    total = d_own + back1.astype(f32) + back2.astype(f32) + back3.astype(f32)
-    total = total + jnp.pad(front.astype(f32), ((0, 0), (0, 384), (0, 0)))
-    total = total.astype(bf16).reshape(2, 4, 128, HD)
-    returned = []
-    for d in range(4):
-        part = lax.dynamic_index_in_dim(total, (x - d) & 3, 1, False)
-        returned.append(along(part, ("section", "ctx_1"), section_route(d, -1)))
-    alike = returned[0].astype(f32) + returned[2].astype(f32)
-    differ = returned[1].astype(f32) + returned[3].astype(f32)
-    low = jnp.where(odd, differ, alike)
-    high = jnp.where(odd, alike, differ)
-    kv_grad = jnp.concatenate([low, high], axis=-1).transpose(1, 0, 2)
+    grad_q = from_units(results[:4], info)
+    totals = combine(info, d_own, back1, back2, back3, front)
+    returned = [
+        along(part, ("section", "ctx_1"), section_route(d, -1))
+        for d, part in enumerate(totals)
+    ]
+    kv_grad = finish(info, returned).transpose(1, 0, 2)
     return normed[None], grad_q[None], kv_grad[None]
 
 

time: 145 us -> 127 us (0.88)
  the two profiles are of different devices: /device:TPU:4 before, /device:TPU:224 now
where the time goes in v3:
time: 127 us
  waiting for transfers between devices  42.3 us (33%)
  Pallas kernels  39.6 us (31%)
  starting transfers between devices  38.7 us (30%)
  local copies, waits for them, and re-layouts  3.3 us (3%)
  other arithmetic  1.7 us (1%)
    ppermute x28, waiting for transfers between devices, along(): return lax.ppermute(x, axis, pairs)  42.3 us
    ppermute x28, starting transfers between devices, along(): return lax.ppermute(x, axis, pairs)  38.7 us
    pallas_call x1, Pallas kernels, forward(): pl.pallas_call(forward_kernel, name='attention_forward', grid_spec=pltpu....  15 us
    pallas_call x1, Pallas kernels, backward_near(): pl.pallas_call(near_kernel, name='backward_near', grid_spec=pltpu.Prefetc...  11.1 us
    pallas_call x1, Pallas kernels, backward_far(): pl.pallas_call(far_kernel, name='backward_far', grid_spec=pltpu.PrefetchS...  8.58 us
    pallas_call x2, Pallas kernels, gather(): pl.pallas_call(gather_kernel, name='gather', in_specs=[SCALARS] + [KEPT]...  2.95 us
  transfers between devices with their start and end apart: 28, of which 14 were waited for; matrix products, arithmetic and copies ran while one was open for 2% of the time, Pallas kernels for 3%

profile of v3, /device:TPU:224, one launch (start us, length us, event | category | flops | bytes accessed | tf_op | source)
XLA Modules:
  0.0 126.7 jit_solution(4508729579005327174)
XLA Ops:
  2.4 3.8 %collective-permute-start.6 = (bf16[272,128]{1,0:T(8,128)(2,1)S(1)}, bf16[272,128]{1,0:T(8,128)(2,1)S(1)}, u32[]{:S(2)}, u32[]{:S(2)}) collective-permute-start(bf16[272,128]{1,0:T(8,128)(2,1)S(1)} %get-tuple-element.66), channel_id=1, source_target_pairs={{0,76},{4,0},{8,4},{12,72},{64,140},{68,64},{72,68},{76,136},{128,... | collective-permute-start | bytes 208904 | tf_op jit(solution)/shard_map/ppermute | solution.py:464
  6.3 4.0 %collective-permute-start.5 = (bf16[272,128]{1,0:T(8,128)(2,1)S(1)}, bf16[272,128]{1,0:T(8,128)(2,1)S(1)}, u32[]{:S(2)}, u32[]{:S(2)}) collective-permute-start(bf16[272,128]{1,0:T(8,128)(2,1)S(1)} %get-tuple-element.67), channel_id=1, source_target_pairs={{0,72},{4,76},{8,0},{12,4},{64,136},{68,140},{72,64},{76,68},{128,... | collective-permute-start | bytes 208904 | tf_op jit(solution)/shard_map/ppermute | solution.py:464
  11.0 1.4 %dynamic-slice_bitcast_fusion = (bf16[128,768]{1,0:T(8,128)(2,1)S(1)}, bf16[128,768]{1,0:T(8,128)(2,1)S(1)}, bf16[128,768]{1,0:T(8,128)(2,1)S(1)}, bf16[128,768]...) fusion(bf16[1,2,128,1536]{3,2,1,0:T(8,128)(2,1)S(1)} %copy-done, ...), kind=kLoop, calls=%fused_computation.4 | loop fusion | bytes 3145760 | tf_op jit(solution)/shard_map/squeeze | solution.py:468
  12.4 2.4 %collective-permute-start.1 = (bf16[256,768]{1,0:T(8,128)(2,1)S(1)}, bf16[256,768]{1,0:T(8,128)(2,1)S(1)}, u32[]{:S(2)}, u32[]{:S(2)}) collective-permute-start(bf16[256,768]{1,0:T(8,128)(2,1)S(1)} %pad_maximum_fusion.2), channel_id=1, source_target_pairs={{0,8},{4,12},{8,0},{12,4},{1,9},{5,13},{9,1},{13,5},{2,10},{6,14},... | collective-permute-start | bytes 1179656 | tf_op jit(solution)/shard_map/ppermute | solution.py:464
  15.5 1.3 %collective-permute-start.9 = (bf16[2,512,128]{2,1,0:T(8,128)(2,1)S(1)}, bf16[2,512,128]{2,1,0:T(8,128)(2,1)S(1)}, u32[]{:S(2)}, u32[]{:S(2)}) collective-permute-start(bf16[2,512,128]{2,1,0:T(8,128)(2,1)S(1)} %get-tuple-element.30.own), channel_id=1, source_target_pairs={{0,32},{16,48},{1,33},{17,49},{2,34},{18,50},{3,35},{19,51},{4,36}... | collective-permute-start | bytes 786440 | tf_op jit(solution)/shard_map/ppermute | solution.py:464
  18.5 2.5 %collective-permute-start.2 = (bf16[256,768]{1,0:T(8,128)(2,1)}, bf16[256,768]{1,0:T(8,128)(2,1)S(1)}, u32[]{:S(2)}, u32[]{:S(2)}) collective-permute-start(bf16[256,768]{1,0:T(8,128)(2,1)} %pad_maximum_fusion.3), channel_id=1, source_target_pairs={{0,12},{4,0},{8,4},{12,8},{1,13},{5,1},{9,5},{13,9},{2,14},{6,2},{... | collective-permute-start | bytes 1179656 | tf_op jit(solution)/shard_map/ppermute | solution.py:464
  21.0 2.9 %collective-permute-start.7 = (bf16[272,128]{1,0:T(8,128)(2,1)S(1)}, bf16[272,128]{1,0:T(8,128)(2,1)S(1)}, u32[]{:S(2)}, u32[]{:S(2)}) collective-permute-start(bf16[272,128]{1,0:T(8,128)(2,1)S(1)} %get-tuple-element.31), channel_id=1, source_target_pairs={{16,0},{32,16},{48,32},{17,1},{33,17},{49,33},{18,2},{34,18},{50,3... | collective-permute-start | bytes 208904 | tf_op jit(solution)/shard_map/ppermute | solution.py:464
  23.9 1.9 %collective-permute-done.7.halo = bf16[272,128]{1,0:T(8,128)(2,1)S(1)} collective-permute-done((bf16[272,128]{1,0:T(8,128)(2,1)S(1)}, bf16[272,128]{1,0:T(8,128)(2,1)S(1)}, u32[]{:S(2)}, u32[]{:S(2)}) %collective-permute-start.7) | collective-permute-done | bytes 69664 | tf_op jit(solution)/shard_map/ppermute | solution.py:464
  27.1 4.3 %collective-permute-done.9.p2 = bf16[2,512,128]{2,1,0:T(8,128)(2,1)S(1)} collective-permute-done((bf16[2,512,128]{2,1,0:T(8,128)(2,1)S(1)}, bf16[2,512,128]{2,1,0:T(8,128)(2,1)S(1)}, u32[]{:S(2)}, u32[]{:S(2)}) %collective-permute-start.9) | collective-permute-done | bytes 262176 | tf_op jit(solution)/shard_map/ppermute | solution.py:464
  31.4 1.3 %collective-permute-start.10 = (bf16[2,512,128]{2,1,0:T(8,128)(2,1)S(1)}, bf16[2,512,128]{2,1,0:T(8,128)(2,1)S(1)}, u32[]{:S(2)}, u32[]{:S(2)}) collective-permute-start(bf16[2,512,128]{2,1,0:T(8,128)(2,1)S(1)} %collective-permute-done.9.p2), channel_id=1, source_target_pairs={{32,48},{33,49},{34,50},{35,51},{36,52},{37,53},{38,54},{39,55},{4... | collective-permute-start | bytes 786440 | tf_op jit(solution)/shard_map/ppermute | solution.py:464
  32.8 5.2 %collective-permute-done.8.p1 = bf16[2,512,128]{2,1,0:T(8,128)(2,1)S(1)} collective-permute-done((bf16[2,512,128]{2,1,0:T(8,128)(2,1)S(1)}, bf16[2,512,128]{2,1,0:T(8,128)(2,1)S(1)}, u32[]{:S(2)}, u32[]{:S(2)}) %collective-permute-start.8) | collective-permute-done | bytes 262176 | tf_op jit(solution)/shard_map/ppermute | solution.py:464
  38.0 4.1 %collective-permute-done.10.p3 = bf16[2,512,128]{2,1,0:T(8,128)(2,1)S(1)} collective-permute-done((bf16[2,512,128]{2,1,0:T(8,128)(2,1)S(1)}, bf16[2,512,128]{2,1,0:T(8,128)(2,1)S(1)}, u32[]{:S(2)}, u32[]{:S(2)}) %collective-permute-start.10) | collective-permute-done | bytes 262176 | tf_op jit(solution)/shard_map/ppermute | solution.py:464
  42.1 15.0 %attention_forward.1 = (f32[6,512,128]{2,1,0:T(8,128)S(1)}, f32[6,512,128]{2,1,0:T(8,128)S(1)}, bf16[6,512,1152]{2,1,0:T(8,128)(2,1)S(1)}, bf16[6,512,1024]{2,1,0:T(8,128)(2,1)S(1)}, f32[8,128]{1,0:T(8,128)S(1)}) custom-call(s32[2]{0:T(128)S(1)} %pad_add_fusion.info, bf16[256,768]{1,0:T(8,128)(2,1)S(1)} %pad_maximum_fusion.q0.g0, ...), custom_call_target="tpu_custom_call" | custom-call | tf_op jit(solution)/shard_map/attention_forward/pallas_call | solution.py:191
  59.1 3.0 %collective-permute-done.12 = f32[8,128]{1,0:T(8,128)S(1)} collective-permute-done((f32[8,128]{1,0:T(8,128)S(1)}, f32[8,128]{1,0:T(8,128)S(1)}, u32[]{:S(2)}, u32[]{:S(2)}) %collective-permute-start.12) | collective-permute-done | bytes 4128 | tf_op jit(solution)/shard_map/ppermute | solution.py:464
  63.1 6.5 %collective-permute-done.13 = f32[8,128]{1,0:T(8,128)S(1)} collective-permute-done((f32[8,128]{1,0:T(8,128)S(1)}, f32[8,128]{1,0:T(8,128)S(1)}, u32[]{:S(2)}, u32[]{:S(2)}) %collective-permute-start.13) | collective-permute-done | bytes 4128 | tf_op jit(solution)/shard_map/ppermute | solution.py:464
  69.7 8.6 %backward_far.1 = (bf16[128,768]{1,0:T(8,128)(2,1)S(1)}, bf16[128,768]{1,0:T(8,128)(2,1)S(1)}, bf16[128,768]{1,0:T(8,128)(2,1)S(1)}, bf16[128,768]{1,0:T(8,128)(...) custom-call(s32[2]{0:T(128)S(1)} %pad_add_fusion.info, ...), custom_call_target="tpu_custom_call" | custom-call | tf_op jit(solution)/shard_map/backward_far/pallas_call | solution.py:303
  78.3 11.1 %backward_near.1 = (bf16[128,768]{1,0:T(8,128)(2,1)S(1)}, bf16[128,768]{1,0:T(8,128)(2,1)S(1)}, bf16[128,768]{1,0:T(8,128)(2,1)S(1)}, bf16[128,768]{1,0:T(8,128)...) custom-call(s32[2]{0:T(128)S(1)} %pad_add_fusion.info, ...), custom_call_target="tpu_custom_call" | custom-call | tf_op jit(solution)/shard_map/backward_near/pallas_call | solution.py:373
  89.4 1.3 %collective-permute-start.20 = (bf16[2,128,512]{2,1,0:T(8,128)(2,1)S(1)}, bf16[2,128,512]{2,1,0:T(8,128)(2,1)S(1)}, u32[]{:S(2)}, u32[]{:S(2)}) collective-permute-start(bf16[2,128,512]{2,1,0:T(8,128)(2,1)S(1)} %get-tuple-element.47), channel_id=1, source_target_pairs={{16,0},{32,16},{48,32},{17,1},{33,17},{49,33},{18,2},{34,18},{50,3... | collective-permute-start | bytes 786440 | tf_op jit(solution)/shard_map/ppermute | solution.py:464
  90.7 1.3 %collective-permute-start.21 = (bf16[2,128,512]{2,1,0:T(8,128)(2,1)S(1)}, bf16[2,128,512]{2,1,0:T(8,128)(2,1)S(1)}, u32[]{:S(2)}, u32[]{:S(2)}) collective-permute-start(bf16[2,128,512]{2,1,0:T(8,128)(2,1)S(1)} %get-tuple-element.48), channel_id=1, source_target_pairs={{32,0},{48,16},{33,1},{49,17},{34,2},{50,18},{35,3},{51,19},{36,4}... | collective-permute-start | bytes 786440 | tf_op jit(solution)/shard_map/ppermute | solution.py:464
  92.0 2.5 %collective-permute-start.14 = (bf16[128,768]{1,0:T(8,128)(2,1)S(1)}, bf16[128,768]{1,0:T(8,128)(2,1)S(1)}, u32[]{:S(2)}, u32[]{:S(2)}) collective-permute-start(bf16[128,768]{1,0:T(8,128)(2,1)S(1)} %get-tuple-element.37), channel_id=1, source_target_pairs={{0,12},{4,0},{8,4},{12,8},{1,13},{5,1},{9,5},{13,9},{2,14},{6,2},{... | collective-permute-start | bytes 589832 | tf_op jit(solution)/shard_map/ppermute | solution.py:464
  94.5 1.3 %collective-permute-start.22 = (bf16[2,128,512]{2,1,0:T(8,128)(2,1)S(1)}, bf16[2,128,512]{2,1,0:T(8,128)(2,1)S(1)}, u32[]{:S(2)}, u32[]{:S(2)}) collective-permute-start(bf16[2,128,512]{2,1,0:T(8,128)(2,1)S(1)} %get-tuple-element.49), channel_id=1, source_target_pairs={{48,0},{49,1},{50,2},{51,3},{52,4},{53,5},{54,6},{55,7},{56,8},{57... | collective-permute-start | bytes 786440 | tf_op jit(solution)/shard_map/ppermute | solution.py:464
  95.8 1.3 %collective-permute-start.23 = (bf16[2,128,128]{2,1,0:T(8,128)(2,1)S(1)}, bf16[2,128,128]{2,1,0:T(8,128)(2,1)S(1)}, u32[]{:S(2)}, u32[]{:S(2)}) collective-permute-start(bf16[2,128,128]{2,1,0:T(8,128)(2,1)S(1)} %get-tuple-element.50), channel_id=1, source_target_pairs={{0,16},{16,32},{32,48},{1,17},{17,33},{33,49},{2,18},{18,34},{34,5... | collective-permute-start | bytes 196616 | tf_op jit(solution)/shard_map/ppermute | solution.py:464
  97.1 4.9 %collective-permute-done.23.front = bf16[2,128,128]{2,1,0:T(8,128)(2,1)S(1)} collective-permute-done((bf16[2,128,128]{2,1,0:T(8,128)(2,1)S(1)}, bf16[2,128,128]{2,1,0:T(8,128)(2,1)S(1)}, u32[]{:S(2)}, u32[]{:S(2)}) %collective-permute-start.23) | collective-permute-done | bytes 65568 | tf_op jit(solution)/shard_map/ppermute | solution.py:464
  103.4 2.1 %collective-permute-start.17 = (bf16[128,768]{1,0:T(8,128)(2,1)S(1)}, bf16[128,768]{1,0:T(8,128)(2,1)S(1)}, u32[]{:S(2)}, u32[]{:S(2)}) collective-permute-start(bf16[128,768]{1,0:T(8,128)(2,1)S(1)} %get-tuple-element.43), channel_id=1, source_target_pairs={{0,12},{4,0},{8,4},{12,8},{1,13},{5,1},{9,5},{13,9},{2,14},{6,2},{... | collective-permute-start | bytes 589832 | tf_op jit(solution)/shard_map/ppermute | solution.py:464
  105.4 2.1 %collective-permute-start.18 = (bf16[128,768]{1,0:T(8,128)(2,1)S(1)}, bf16[128,768]{1,0:T(8,128)(2,1)S(1)}, u32[]{:S(2)}, u32[]{:S(2)}) collective-permute-start(bf16[128,768]{1,0:T(8,128)(2,1)S(1)} %get-tuple-element.44), channel_id=1, source_target_pairs={{0,8},{4,12},{8,0},{12,4},{1,9},{5,13},{9,1},{13,5},{2,10},{6,14},... | collective-permute-start | bytes 589832 | tf_op jit(solution)/shard_map/ppermute | solution.py:464
  108.3 3.0 %collective-permute-done.15.r2 = bf16[128,768]{1,0:T(8,128)(2,1)S(1)} collective-permute-done((bf16[128,768]{1,0:T(8,128)(2,1)S(1)}, bf16[128,768]{1,0:T(8,128)(2,1)S(1)}, u32[]{:S(2)}, u32[]{:S(2)}) %collective-permute-start.15) | collective-permute-done | bytes 196640 | tf_op jit(solution)/shard_map/ppermute | solution.py:464
  112.0 3.5 %collective-permute-done.16.r3 = bf16[128,768]{1,0:T(8,128)(2,1)S(1)} collective-permute-done((bf16[128,768]{1,0:T(8,128)(2,1)S(1)}, bf16[128,768]{1,0:T(8,128)(2,1)S(1)}, u32[]{:S(2)}, u32[]{:S(2)}) %collective-permute-start.16) | collective-permute-done | bytes 196640 | tf_op jit(solution)/shard_map/ppermute | solution.py:464
  116.1 1.3 %collective-permute-start.26 = (bf16[2,128,128]{2,1,0:T(8,128)(2,1)S(1)}, bf16[2,128,128]{2,1,0:T(8,128)(2,1)S(1)}, u32[]{:S(2)}, u32[]{:S(2)}) collective-permute-start(bf16[2,128,128]{2,1,0:T(8,128)(2,1)S(1)} %get-tuple-element.53), channel_id=1, source_target_pairs={{0,8},{4,12},{8,192},{12,196},{64,72},{68,76},{72,0},{76,4},{128,1... | collective-permute-start | bytes 196616 | tf_op jit(solution)/shard_map/ppermute | solution.py:464
  117.4 1.3 %collective-permute-done.18.r2 = bf16[128,768]{1,0:T(8,128)(2,1)S(1)} collective-permute-done((bf16[128,768]{1,0:T(8,128)(2,1)S(1)}, bf16[128,768]{1,0:T(8,128)(2,1)S(1)}, u32[]{:S(2)}, u32[]{:S(2)}) %collective-permute-start.18) | collective-permute-done | bytes 196640 | tf_op jit(solution)/shard_map/ppermute | solution.py:464
  118.8 1.5 %gather.2 = bf16[2,128,1536]{2,1,0:T(8,128)(2,1)} custom-call(s32[2]{0:T(128)S(1)} %pad_add_fusion.info, bf16[128,768]{1,0:T(8,128)(2,1)S(1)} %get-tuple-element.36.r0, bf16[128,768]{1,0:T(8,128)(2,1)S(1)} %collective-permute-done.14.r1, bf16[128,768]{1,0:T(8,128)(2,1)S(1)} %collective-permute-done.15.r2, bf16[128,768]{1,0:T(8,128)(2,1)S(1)} %collective-permute-done.16.r3), custom_call_target="tpu_custom_call" | custom-call | tf_op jit(solution)/shard_map/gather/pallas_call | solution.py:453
  120.8 1.5 %gather.3 = bf16[2,128,1536]{2,1,0:T(8,128)(2,1)} custom-call(s32[2]{0:T(128)S(1)} %pad_add_fusion.info, bf16[128,768]{1,0:T(8,128)(2,1)S(1)} %get-tuple-element.42.r0, bf16[128,768]{1,0:T(8,128)(2,1)S(1)} %collective-permute-done.17.r1, bf16[128,768]{1,0:T(8,128)(2,1)S(1)} %collective-permute-done.18.r2, bf16[128,768]{1,0:T(8,128)(2,1)S(1)} %collective-permute-done.19.r3), custom_call_target="tpu_custom_call" | custom-call | tf_op jit(solution)/shard_map/gather/pallas_call | solution.py:453
  122.7 2.4 %collective-permute-done.27.r3 = bf16[2,128,128]{2,1,0:T(8,128)(2,1)S(1)} collective-permute-done((bf16[2,128,128]{2,1,0:T(8,128)(2,1)S(1)}, bf16[2,128,128]{2,1,0:T(8,128)(2,1)S(1)}, u32[]{:S(2)}, u32[]{:S(2)}) %collective-permute-start.27) | collective-permute-done | bytes 65568 | tf_op jit(solution)/shard_map/ppermute | solution.py:464
  (52 shorter events, 15.2 us)
Async XLA Ops:
  0.6 32.0 %copy-start = (f32[1,2,1536]{2,1,0:T(2,128)S(1)}, f32[1,2,1536]{2,1,0:T(2,128)}, u32[]{:S(2)}) copy-start(f32[1,2,1536]{2,1,0:T(2,128)} %param.8) | copy-start | bytes 36868
  0.6 10.4 %copy-start.1 = (bf16[1,2,128,1536]{3,2,1,0:T(8,128)(2,1)S(1)}, bf16[1,2,128,1536]{3,2,1,0:T(8,128)(2,1)}, u32[]{:S(2)}) copy-start(bf16[1,2,128,1536]{3,2,1,0:T(8,128)(2,1)} %param.7) | copy-start | bytes 2359300
  2.4 12.5 %collective-permute-start.6 = (bf16[272,128]{1,0:T(8,128)(2,1)S(1)}, bf16[272,128]{1,0:T(8,128)(2,1)S(1)}, u32[]{:S(2)}, u32[]{:S(2)}) collective-permute-start(bf16[272,128]{1,0:T(8,128)(2,1)S(1)} %get-tuple-element.66), channel_id=1, source_target_pairs={{0,76},{4,0},{8,4},{12,72},{64,140},{68,64},{72,68},{76,136},{128,... | collective-permute-start | bytes 208904 | tf_op jit(solution)/shard_map/ppermute | solution.py:464
  6.3 8.7 %collective-permute-start.4 = (bf16[272,128]{1,0:T(8,128)(2,1)S(1)}, bf16[272,128]{1,0:T(8,128)(2,1)S(1)}, u32[]{:S(2)}, u32[]{:S(2)}) collective-permute-start(bf16[272,128]{1,0:T(8,128)(2,1)S(1)} %get-tuple-element.66), channel_id=1, source_target_pairs={{0,4},{4,72},{8,76},{12,0},{64,68},{68,136},{72,140},{76,64},{128,... | collective-permute-start | bytes 208904 | tf_op jit(solution)/shard_map/ppermute | solution.py:464
  6.3 8.7 %collective-permute-start.5 = (bf16[272,128]{1,0:T(8,128)(2,1)S(1)}, bf16[272,128]{1,0:T(8,128)(2,1)S(1)}, u32[]{:S(2)}, u32[]{:S(2)}) collective-permute-start(bf16[272,128]{1,0:T(8,128)(2,1)S(1)} %get-tuple-element.67), channel_id=1, source_target_pairs={{0,72},{4,76},{8,0},{12,4},{64,136},{68,140},{72,64},{76,68},{128,... | collective-permute-start | bytes 208904 | tf_op jit(solution)/shard_map/ppermute | solution.py:464
  10.3 4.7 %collective-permute-start.3 = (bf16[272,128]{1,0:T(8,128)(2,1)S(1)}, bf16[272,128]{1,0:T(8,128)(2,1)S(1)}, u32[]{:S(2)}, u32[]{:S(2)}) collective-permute-start(bf16[272,128]{1,0:T(8,128)(2,1)S(1)} %get-tuple-element.67), channel_id=1, source_target_pairs={{0,0},{4,4},{8,72},{12,76},{64,64},{68,68},{72,136},{76,140},{128,... | collective-permute-start | bytes 208904 | tf_op jit(solution)/shard_map/ppermute | solution.py:464
  12.4 25.5 %collective-permute-start.1 = (bf16[256,768]{1,0:T(8,128)(2,1)S(1)}, bf16[256,768]{1,0:T(8,128)(2,1)S(1)}, u32[]{:S(2)}, u32[]{:S(2)}) collective-permute-start(bf16[256,768]{1,0:T(8,128)(2,1)S(1)} %pad_maximum_fusion.2), channel_id=1, source_target_pairs={{0,8},{4,12},{8,0},{12,4},{1,9},{5,13},{9,1},{13,5},{2,10},{6,14},... | collective-permute-start | bytes 1179656 | tf_op jit(solution)/shard_map/ppermute | solution.py:464
  15.5 15.8 %collective-permute-start.9 = (bf16[2,512,128]{2,1,0:T(8,128)(2,1)S(1)}, bf16[2,512,128]{2,1,0:T(8,128)(2,1)S(1)}, u32[]{:S(2)}, u32[]{:S(2)}) collective-permute-start(bf16[2,512,128]{2,1,0:T(8,128)(2,1)S(1)} %get-tuple-element.30.own), channel_id=1, source_target_pairs={{0,32},{16,48},{1,33},{17,49},{2,34},{18,50},{3,35},{19,51},{4,36}... | collective-permute-start | bytes 786440 | tf_op jit(solution)/shard_map/ppermute | solution.py:464
  16.9 21.1 %collective-permute-start = (bf16[256,768]{1,0:T(8,128)(2,1)S(1)}, bf16[256,768]{1,0:T(8,128)(2,1)S(1)}, u32[]{:S(2)}, u32[]{:S(2)}) collective-permute-start(bf16[256,768]{1,0:T(8,128)(2,1)S(1)} %pad_maximum_fusion.1), channel_id=1, source_target_pairs={{0,4},{4,8},{8,12},{12,0},{1,5},{5,9},{9,13},{13,1},{2,6},{6,10},{... | collective-permute-start | bytes 1179656 | tf_op jit(solution)/shard_map/ppermute | solution.py:464
  18.5 19.5 %collective-permute-start.2 = (bf16[256,768]{1,0:T(8,128)(2,1)}, bf16[256,768]{1,0:T(8,128)(2,1)S(1)}, u32[]{:S(2)}, u32[]{:S(2)}) collective-permute-start(bf16[256,768]{1,0:T(8,128)(2,1)} %pad_maximum_fusion.3), channel_id=1, source_target_pairs={{0,12},{4,0},{8,4},{12,8},{1,13},{5,1},{9,5},{13,9},{2,14},{6,2},{... | collective-permute-start | bytes 1179656 | tf_op jit(solution)/shard_map/ppermute | solution.py:464
  21.0 4.8 %collective-permute-start.7 = (bf16[272,128]{1,0:T(8,128)(2,1)S(1)}, bf16[272,128]{1,0:T(8,128)(2,1)S(1)}, u32[]{:S(2)}, u32[]{:S(2)}) collective-permute-start(bf16[272,128]{1,0:T(8,128)(2,1)S(1)} %get-tuple-element.31), channel_id=1, source_target_pairs={{16,0},{32,16},{48,32},{17,1},{33,17},{49,33},{18,2},{34,18},{50,3... | collective-permute-start | bytes 208904 | tf_op jit(solution)/shard_map/ppermute | solution.py:464
  25.8 12.2 %collective-permute-start.8 = (bf16[2,512,128]{2,1,0:T(8,128)(2,1)S(1)}, bf16[2,512,128]{2,1,0:T(8,128)(2,1)S(1)}, u32[]{:S(2)}, u32[]{:S(2)}) collective-permute-start(bf16[2,512,128]{2,1,0:T(8,128)(2,1)S(1)} %get-tuple-element.30.own), channel_id=1, source_target_pairs={{0,16},{16,32},{32,48},{1,17},{17,33},{33,49},{2,18},{18,34},{34,5... | collective-permute-start | bytes 786440 | tf_op jit(solution)/shard_map/ppermute | solution.py:464
  31.4 10.8 %collective-permute-start.10 = (bf16[2,512,128]{2,1,0:T(8,128)(2,1)S(1)}, bf16[2,512,128]{2,1,0:T(8,128)(2,1)S(1)}, u32[]{:S(2)}, u32[]{:S(2)}) collective-permute-start(bf16[2,512,128]{2,1,0:T(8,128)(2,1)S(1)} %collective-permute-done.9.p2), channel_id=1, source_target_pairs={{32,48},{33,49},{34,50},{35,51},{36,52},{37,53},{38,54},{39,55},{4... | collective-permute-start | bytes 786440 | tf_op jit(solution)/shard_map/ppermute | solution.py:464
  57.1 1.4 %collective-permute-start.11 = (f32[8,128]{1,0:T(8,128)S(1)}, f32[8,128]{1,0:T(8,128)S(1)}, u32[]{:S(2)}, u32[]{:S(2)}) collective-permute-start(f32[8,128]{1,0:T(8,128)S(1)} %get-tuple-element.32), channel_id=1, source_target_pairs={{0,1},{1,0},{2,3},{3,2},{4,5},{5,4},{6,7},{7,6},{8,9},{9,8},{10,11... | collective-permute-start | bytes 12296 | tf_op jit(solution)/shard_map/ppermute | solution.py:464
  58.6 3.6 %collective-permute-start.12 = (f32[8,128]{1,0:T(8,128)S(1)}, f32[8,128]{1,0:T(8,128)S(1)}, u32[]{:S(2)}, u32[]{:S(2)}) collective-permute-start(f32[8,128]{1,0:T(8,128)S(1)} %add.99), channel_id=1, source_target_pairs={{0,4},{4,0},{8,12},{12,8},{1,5},{5,1},{9,13},{13,9},{2,6},{6,2},{1... | collective-permute-start | bytes 12296 | tf_op jit(solution)/shard_map/ppermute | solution.py:464
  62.2 7.5 %collective-permute-start.13 = (f32[8,128]{1,0:T(8,128)S(1)}, f32[8,128]{1,0:T(8,128)S(1)}, u32[]{:S(2)}, u32[]{:S(2)}) collective-permute-start(f32[8,128]{1,0:T(8,128)S(1)} %add.100), channel_id=1, source_target_pairs={{0,2},{1,3},{2,0},{3,1},{4,6},{5,7},{6,4},{7,5},{8,10},{9,11},{10,... | collective-permute-start | bytes 12296 | tf_op jit(solution)/shard_map/ppermute | solution.py:464
  89.4 14.0 %collective-permute-start.20 = (bf16[2,128,512]{2,1,0:T(8,128)(2,1)S(1)}, bf16[2,128,512]{2,1,0:T(8,128)(2,1)S(1)}, u32[]{:S(2)}, u32[]{:S(2)}) collective-permute-start(bf16[2,128,512]{2,1,0:T(8,128)(2,1)S(1)} %get-tuple-element.47), channel_id=1, source_target_pairs={{16,0},{32,16},{48,32},{17,1},{33,17},{49,33},{18,2},{34,18},{50,3... | collective-permute-start | bytes 786440 | tf_op jit(solution)/shard_map/ppermute | solution.py:464
  90.7 14.8 %collective-permute-start.21 = (bf16[2,128,512]{2,1,0:T(8,128)(2,1)S(1)}, bf16[2,128,512]{2,1,0:T(8,128)(2,1)S(1)}, u32[]{:S(2)}, u32[]{:S(2)}) collective-permute-start(bf16[2,128,512]{2,1,0:T(8,128)(2,1)S(1)} %get-tuple-element.48), channel_id=1, source_target_pairs={{32,0},{48,16},{33,1},{49,17},{34,2},{50,18},{35,3},{51,19},{36,4}... | collective-permute-start | bytes 786440 | tf_op jit(solution)/shard_map/ppermute | solution.py:464
  92.0 10.2 %collective-permute-start.14 = (bf16[128,768]{1,0:T(8,128)(2,1)S(1)}, bf16[128,768]{1,0:T(8,128)(2,1)S(1)}, u32[]{:S(2)}, u32[]{:S(2)}) collective-permute-start(bf16[128,768]{1,0:T(8,128)(2,1)S(1)} %get-tuple-element.37), channel_id=1, source_target_pairs={{0,12},{4,0},{8,4},{12,8},{1,13},{5,1},{9,5},{13,9},{2,14},{6,2},{... | collective-permute-start | bytes 589832 | tf_op jit(solution)/shard_map/ppermute | solution.py:464
  94.5 13.0 %collective-permute-start.22 = (bf16[2,128,512]{2,1,0:T(8,128)(2,1)S(1)}, bf16[2,128,512]{2,1,0:T(8,128)(2,1)S(1)}, u32[]{:S(2)}, u32[]{:S(2)}) collective-permute-start(bf16[2,128,512]{2,1,0:T(8,128)(2,1)S(1)} %get-tuple-element.49), channel_id=1, source_target_pairs={{48,0},{49,1},{50,2},{51,3},{52,4},{53,5},{54,6},{55,7},{56,8},{57... | collective-permute-start | bytes 786440 | tf_op jit(solution)/shard_map/ppermute | solution.py:464
  95.8 6.2 %collective-permute-start.23 = (bf16[2,128,128]{2,1,0:T(8,128)(2,1)S(1)}, bf16[2,128,128]{2,1,0:T(8,128)(2,1)S(1)}, u32[]{:S(2)}, u32[]{:S(2)}) collective-permute-start(bf16[2,128,128]{2,1,0:T(8,128)(2,1)S(1)} %get-tuple-element.50), channel_id=1, source_target_pairs={{0,16},{16,32},{32,48},{1,17},{17,33},{33,49},{2,18},{18,34},{34,5... | collective-permute-start | bytes 196616 | tf_op jit(solution)/shard_map/ppermute | solution.py:464
  102.0 9.3 %collective-permute-start.15 = (bf16[128,768]{1,0:T(8,128)(2,1)S(1)}, bf16[128,768]{1,0:T(8,128)(2,1)S(1)}, u32[]{:S(2)}, u32[]{:S(2)}) collective-permute-start(bf16[128,768]{1,0:T(8,128)(2,1)S(1)} %get-tuple-element.38), channel_id=1, source_target_pairs={{0,8},{4,12},{8,0},{12,4},{1,9},{5,13},{9,1},{13,5},{2,10},{6,14},... | collective-permute-start | bytes 589832 | tf_op jit(solution)/shard_map/ppermute | solution.py:464
  102.2 13.2 %collective-permute-start.16 = (bf16[128,768]{1,0:T(8,128)(2,1)S(1)}, bf16[128,768]{1,0:T(8,128)(2,1)S(1)}, u32[]{:S(2)}, u32[]{:S(2)}) collective-permute-start(bf16[128,768]{1,0:T(8,128)(2,1)S(1)} %get-tuple-element.39), channel_id=1, source_target_pairs={{0,4},{4,8},{8,12},{12,0},{1,5},{5,9},{9,13},{13,1},{2,6},{6,10},{... | collective-permute-start | bytes 589832 | tf_op jit(solution)/shard_map/ppermute | solution.py:464
  103.4 12.7 %collective-permute-start.17 = (bf16[128,768]{1,0:T(8,128)(2,1)S(1)}, bf16[128,768]{1,0:T(8,128)(2,1)S(1)}, u32[]{:S(2)}, u32[]{:S(2)}) collective-permute-start(bf16[128,768]{1,0:T(8,128)(2,1)S(1)} %get-tuple-element.43), channel_id=1, source_target_pairs={{0,12},{4,0},{8,4},{12,8},{1,13},{5,1},{9,5},{13,9},{2,14},{6,2},{... | collective-permute-start | bytes 589832 | tf_op jit(solution)/shard_map/ppermute | solution.py:464
  105.4 13.3 %collective-permute-start.18 = (bf16[128,768]{1,0:T(8,128)(2,1)S(1)}, bf16[128,768]{1,0:T(8,128)(2,1)S(1)}, u32[]{:S(2)}, u32[]{:S(2)}) collective-permute-start(bf16[128,768]{1,0:T(8,128)(2,1)S(1)} %get-tuple-element.44), channel_id=1, source_target_pairs={{0,8},{4,12},{8,0},{12,4},{1,9},{5,13},{9,1},{13,5},{2,10},{6,14},... | collective-permute-start | bytes 589832 | tf_op jit(solution)/shard_map/ppermute | solution.py:464
  107.5 13.3 %collective-permute-start.19 = (bf16[128,768]{1,0:T(8,128)(2,1)S(1)}, bf16[128,768]{1,0:T(8,128)(2,1)S(1)}, u32[]{:S(2)}, u32[]{:S(2)}) collective-permute-start(bf16[128,768]{1,0:T(8,128)(2,1)S(1)} %get-tuple-element.45), channel_id=1, source_target_pairs={{0,4},{4,8},{8,12},{12,0},{1,5},{5,9},{9,13},{13,1},{2,6},{6,10},{... | collective-permute-start | bytes 589832 | tf_op jit(solution)/shard_map/ppermute | solution.py:464
  111.3 11.0 %collective-permute-start.24 = (bf16[2,128,128]{2,1,0:T(8,128)(2,1)S(1)}, bf16[2,128,128]{2,1,0:T(8,128)(2,1)S(1)}, u32[]{:S(2)}, u32[]{:S(2)}) collective-permute-start(bf16[2,128,128]{2,1,0:T(8,128)(2,1)S(1)} %get-tuple-element.51), channel_id=1, source_target_pairs={{0,0},{4,4},{8,200},{12,204},{64,64},{68,68},{72,8},{76,12},{128,1... | collective-permute-start | bytes 196616 | tf_op jit(solution)/shard_map/ppermute | solution.py:464
  115.4 6.9 %collective-permute-start.25 = (bf16[2,128,128]{2,1,0:T(8,128)(2,1)S(1)}, bf16[2,128,128]{2,1,0:T(8,128)(2,1)S(1)}, u32[]{:S(2)}, u32[]{:S(2)}) collective-permute-start(bf16[2,128,128]{2,1,0:T(8,128)(2,1)S(1)} %get-tuple-element.52), channel_id=1, source_target_pairs={{0,12},{4,0},{8,196},{12,200},{64,76},{68,64},{72,4},{76,8},{128,1... | collective-permute-start | bytes 196616 | tf_op jit(solution)/shard_map/ppermute | solution.py:464
  116.1 6.7 %collective-permute-start.26 = (bf16[2,128,128]{2,1,0:T(8,128)(2,1)S(1)}, bf16[2,128,128]{2,1,0:T(8,128)(2,1)S(1)}, u32[]{:S(2)}, u32[]{:S(2)}) collective-permute-start(bf16[2,128,128]{2,1,0:T(8,128)(2,1)S(1)} %get-tuple-element.53), channel_id=1, source_target_pairs={{0,8},{4,12},{8,192},{12,196},{64,72},{68,76},{72,0},{76,4},{128,1... | collective-permute-start | bytes 196616 | tf_op jit(solution)/shard_map/ppermute | solution.py:464
  118.7 6.4 %collective-permute-start.27 = (bf16[2,128,128]{2,1,0:T(8,128)(2,1)S(1)}, bf16[2,128,128]{2,1,0:T(8,128)(2,1)S(1)}, u32[]{:S(2)}, u32[]{:S(2)}) collective-permute-start(bf16[2,128,128]{2,1,0:T(8,128)(2,1)S(1)} %get-tuple-element.54), channel_id=1, source_target_pairs={{0,4},{4,8},{8,204},{12,192},{64,68},{68,72},{72,12},{76,0},{128,1... | collective-permute-start | bytes 196616 | tf_op jit(solution)/shard_map/ppermute | solution.py:464
